TPU v7x, 256 devices: a whole 4x4x8 slice. The times are simulated.
256 devices in a mesh: dp: 8 (over y, x_lo), tensor: 32 (over x_hi, z, core).
Axes of the slice: x: 4 (x_hi: 2, x_lo: 2; x = x_hi * 2 + x_lo), y: 4, z: 8, core: 2. Of those that a mesh axis runs over, the one named last changes fastest.
Arguments:
- hidden: bfloat16 [6144, 20480], P('dp', 'tensor'), may hold values from -6 to 6
- out_grad: bfloat16 [6144, 8192], P('dp', 'tensor'), may hold values from -6 to 6
- w_down: bfloat16 [20480, 8192], P('tensor'), may hold values from -0.0625 to 0.0625
- proj_in: bfloat16 [64, 20480], P(None, 'tensor'), may hold values from -0.0390625 to 0.0390625
- proj_out: bfloat16 [64, 8192], P(None, 'tensor'), may hold values from -0.0625 to 0.0625
- queries: bfloat16 [1024, 4096], P('tensor'), may hold values from -0.005859375 to 0.005859375
- assignment: int32 [24], replicated, may hold values from 0 to 15
Outputs:
- input_grad: bfloat16 [6144, 20480], P('dp', 'tensor')
- scores: float32 [16, 1024], P('dp', 'tensor')
All inputs are finite; a program needn't handle non-finite values.
Results may differ from a plain program's by a relative error of at most 0.001.
Values may be sent and summed in bfloat16 or wider, within the bound.
No kernel may reach another device: no remote copies, remote signals or barrier semaphores. Data moves between devices by JAX's collectives and lax.ppermute only.
A program may use at most 128 MiB of HBM per device.

v0:
```python
import jax
import jax.numpy as jnp
from jax import lax
from jax.sharding import PartitionSpec as P

LEN = 256
EX_DEV = 2


def on_device(hidden, out_grad, w_down, proj_in, proj_out, queries, assignment):
    tok_rows = hidden.shape[0]
    seq_count = tok_rows // LEN
    act_part = jnp.einsum("tf,kf->tk", hidden, proj_in, preferred_element_type=jnp.float32)
    grad_piece = lax.all_gather(out_grad, "tensor", axis=1, tiled=True)
    proj_piece = lax.all_gather(proj_out, "tensor", axis=1, tiled=True)
    first = jnp.einsum("td,fd->tf", grad_piece, w_down, preferred_element_type=jnp.float32)
    second = jnp.einsum("td,kd->tk", grad_piece, proj_piece, preferred_element_type=jnp.float32)
    act_low = lax.psum(act_part, "tensor")
    input_grad = first.astype(jnp.bfloat16)
    width = act_low.shape[1]
    act_seq = act_low.reshape(seq_count, LEN, width)
    grad_seq = second.reshape(seq_count, LEN, width)
    proj_grads = jnp.einsum(
        "slk,slm->skm", act_seq, grad_seq, precision=lax.Precision.HIGHEST
    ).reshape(seq_count, width * width)
    query_wide = queries.astype(jnp.float32)
    all_grads = lax.all_gather(proj_grads, "dp", axis=0, tiled=True)
    first_example = lax.axis_index("dp") * EX_DEV
    example_ids = first_example + jnp.arange(EX_DEV, dtype=jnp.int32)
    one_hot = (example_ids[:, None] == assignment[None, :]).astype(jnp.float32)
    example_grads = jnp.dot(one_hot, all_grads, precision=lax.Precision.HIGHEST)
    scores = jnp.dot(example_grads, query_wide.T, precision=lax.Precision.HIGHEST)
    return (input_grad, scores)


def solution(mesh):
    placed = (
        P("dp", "tensor"),
        P("dp", "tensor"),
        P("tensor", None),
        P(None, "tensor"),
        P(None, "tensor"),
        P("tensor", None),
        P(),
    )
    return jax.shard_map(
        on_device,
        mesh=mesh,
        in_specs=placed,
        out_specs=(P("dp", "tensor"), P("dp", "tensor")),
        check_vma=False,
    )
```

profile of v0, /device:TPU:1, one launch (start us, length us, event | category | flops | bytes accessed | tf_op | source)
XLA Modules:
  0.0 518.4 jit_solution(11781420502975008039)
XLA Ops:
  7.2 0.0 copy-start
  7.2 0.0 copy-start.1
  7.2 0.0 copy-start.2
  7.2 0.0 all-gather.6.cloned.1.call-start
  7.2 0.7 all-gather.6.cloned.1.call-update
  7.9 0.0 all-gather.4.cloned.1.call-start
  8.0 0.7 all-gather.4.cloned.1.call-update
  8.7 0.0 all-reduce.2.cloned.1.call-start
  8.7 0.0 copy-done
  8.7 1.3 fusion.7
  10.0 0.7 copy.22
  10.7 0.0 all-reduce.2.cloned.1.call-update
  10.8 76.1 %all-gather.6.cloned.1.call-done = bf16[64,8192]{1,0:T(8,128)(2,1)} async-done(((bf16[64,256]{1,0:T(8,128)(2,1)}), bf16[64,8192]{1,0:T(8,128)(2,1)}) %all-gather.6.cloned.1.call-update) | async-done | bytes 1048592 | tf_op jit(solution)/shard_map/all_gather | solution.py:15
  86.9 130.4 %all-gather.4.cloned.1.call-done = bf16[768,8192]{1,0:T(8,128)(2,1)} async-done(((bf16[768,256]{1,0:T(8,128)(2,1)}), bf16[768,8192]{1,0:T(8,128)(2,1)}) %all-gather.4.cloned.1.call-update) | async-done | bytes 12582928 | tf_op jit(solution)/shard_map/all_gather | solution.py:14
  217.2 8.7 %fusion.8 = f32[768,64]{0,1:T(8,128)S(1)} fusion(bf16[768,8192]{1,0:T(8,128)(2,1)} %all-gather.4.cloned.1.call-done, bf16[64,8192]{1,0:T(8,128)(2,1)} %all-gather.6.cloned.1.call-done), kind=kOutput, calls=%fused_computation.11 | convolution fusion | flops 805306368 | bytes 13828096 | tf_op jit(solution)/shard_map/td,kd->tk/dot_general | solution.py:17
  226.0 243.0 %all-reduce.2.cloned.1.call-done = f32[3,256,64]{1,2,0:T(8,128)} async-done(((f32[3,256,64]{1,2,0:T(8,128)}), f32[3,256,64]{1,2,0:T(8,128)}) %all-reduce.2.cloned.1.call-update) | async-done | bytes 196624 | tf_op jit(solution)/shard_map/psum | solution.py:18
  469.0 1.2 fusion
  470.3 0.1 reshape.21
  470.4 24.6 %all-gather = f32[8,3,4096]{2,1,0:T(4,128)S(1)} all-gather(f32[1,3,4096]{2,1,0:T(4,128)S(1)} %reshape.21), channel_id=1, replica_groups=mesh['dp'=8,'tensor'=32] {'dp'}, dimensions={0}, use_global_device_ids=true | all-gather | bytes 442368 | tf_op jit(solution)/shard_map/all_gather | solution.py:27
  495.0 0.2 reshape.22
  495.2 0.0 copy-done.1
  495.2 0.3 fusion.3
  495.5 0.0 copy-done.2
  495.5 0.9 fusion.9
  496.4 15.5 %convolution_convert_fusion = bf16[768,640]{1,0:T(8,128)(2,1)} fusion(bf16[768,8192]{1,0:T(8,128)(2,1)} %all-gather.4.cloned.1.call-done, bf16[640,8192]{1,0:T(8,128)(2,1)} %param.9), kind=kOutput, calls=%fused_computation | convolution fusion | flops 8053555200 | bytes 24051712 | tf_op jit(solution)/shard_map/td,fd->tf/dot_general | solution.py:16
  (1 shorter events, 0.0 us)
Async XLA Ops:
  7.2 1.6 copy-start
  7.2 488.0 %copy-start.1 = (s32[24]{0:T(128)S(1)}, s32[24]{0:T(128)}, u32[]{:S(2)}) copy-start(s32[24]{0:T(128)} %param.13) | copy-start | bytes 292
  7.2 488.3 %copy-start.2 = (bf16[32,4096]{1,0:T(8,128)(2,1)S(1)}, bf16[32,4096]{1,0:T(8,128)(2,1)}, u32[]{:S(2)}) copy-start(bf16[32,4096]{1,0:T(8,128)(2,1)} %param.12) | copy-start | bytes 786436
  7.2 79.7 %all-gather.6.cloned.1.call-start = ((), (), s32[]{:S(2)}) async-start(), calls=%async_computation.2 | async-start | bytes 1081344 | tf_op jit(solution)/shard_map/all_gather | solution.py:15
  7.9 209.3 %all-gather.4.cloned.1.call-start = ((), (), s32[]{:S(2)}) async-start(), calls=%async_computation | async-start | bytes 12976128 | tf_op jit(solution)/shard_map/all_gather | solution.py:14
  8.7 460.3 %all-reduce.2.cloned.1.call-start = ((), (), s32[]{:S(2)}) async-start(), calls=%async_computation.1 | async-start | bytes 393216 | tf_op jit(solution)/shard_map/psum | solution.py:18
Sparse Core Ops, SparseCore 0:
  10.6 76.2 all-gather.5
  89.4 127.7 all-gather.3
  220.4 248.5 all-reduce.1
where the time goes:
time: 525 us; the launch traced here: 518 us
  waiting for transfers between devices  451 us (86%)
  matrix products  27.9 us (5%)
  blocking collectives  24.6 us (5%)
  between operations  13.8 us (3%)
    psum x1, waiting for transfers between devices, on_device(): act_low = lax.psum(act_part, 'tensor')  243 us
    all_gather x1, waiting for transfers between devices, on_device(): grad_piece = lax.all_gather(out_grad, 'tensor', axis=1, tiled=True)  130 us
    all_gather x1, waiting for transfers between devices, on_device(): proj_piece = lax.all_gather(proj_out, 'tensor', axis=1, tiled=True)  76.1 us
    all_gather x1, blocking collectives, on_device(): all_grads = lax.all_gather(proj_grads, 'dp', axis=0, tiled=True)  24.6 us
    dot_general x1, matrix products, on_device(): jnp.einsum('td,fd->tf', grad_piece, w_down, preferred_element_type=jnp.fl...  15.5 us
  transfers between devices with their start and end apart: 3, of which 3 were waited for; matrix products, arithmetic and copies ran while one was open for 2% of the time, Pallas kernels for 0%

commit v1 on v0

v1 whole, which is shorter than its diff:
```python
import jax
import jax.numpy as jnp
from jax import lax
from jax.sharding import PartitionSpec as P

LEN = 256
EX_DEV = 2
DP = 8
TENSOR = 32
ZN = 8


def place(xh, z, c):
    return xh * 16 + (z % ZN) * 2 + c


def pairs(move):
    out = []
    for xh in range(2):
        for z in range(ZN):
            for c in range(2):
                out.append((place(xh, z, c), place(*move(xh, z, c))))
    return out


CORE = pairs(lambda xh, z, c: (xh, z, 1 - c))
ACROSS = pairs(lambda xh, z, c: (1 - xh, z, c))
ALONG = pairs(lambda xh, z, c: (xh, z + 1 - 2 * c, c))
Z_GROUPS = [[place(xh, z, c) for z in range(ZN)] for xh in range(2) for c in range(2)]


def move(value, perm):
    return lax.ppermute(value, "tensor", perm)


def mul(rows, weights):
    return lax.dot_general(rows, weights, (((1,), (1,)), ((), ())), preferred_element_type=jnp.float32)


def on_device(hidden, out_grad, w_down, proj_in, proj_out, queries, assignment):
    rank = lax.axis_index("tensor")
    core = rank & 1
    z = (rank >> 1) & (ZN - 1)
    xh = rank >> 4
    toward = 1 - 2 * core
    width = out_grad.shape[1]

    def weights(column, depth):
        chip = column * ZN + ((depth + 2 * ZN) & (ZN - 1))
        return lax.dynamic_slice(w_down, (0, chip * 2 * width), (w_down.shape[0], 2 * width))

    def both(own, other):
        return jnp.where(core == 0, jnp.concatenate([own, other], 1), jnp.concatenate([other, own], 1))

    own_col = both(out_grad, move(out_grad, CORE))
    crossed = move(out_grad, ACROSS)
    other_col = both(crossed, move(crossed, CORE))

    act_part = mul(hidden, proj_in)
    grad_part = mul(out_grad, proj_out)
    low = jnp.concatenate([act_part, grad_part], 1)
    seq_count = low.shape[0] // LEN
    wide = low.shape[1]
    low = low.reshape(seq_count, LEN, wide)

    def halve(value, bit, perm):
        half = value.shape[1] // 2
        keep = lax.dynamic_slice_in_dim(value, bit * half, half, 1)
        give = lax.dynamic_slice_in_dim(value, (1 - bit) * half, half, 1)
        return keep + move(give, perm)

    low = halve(low, core, CORE)
    low = halve(low, xh, ACROSS)
    share = low.shape[1] // ZN
    low = low.reshape(seq_count, ZN, share, wide).transpose(1, 0, 2, 3)
    low = lax.all_to_all(low, "tensor", 0, 0, axis_index_groups=Z_GROUPS, tiled=True)
    low = jnp.sum(low, 0)
    low = jnp.broadcast_to(low[None], (ZN,) + low.shape)
    low = lax.all_to_all(low, "tensor", 0, 0, axis_index_groups=Z_GROUPS, tiled=True)
    low = low.transpose(1, 0, 2, 3).reshape(seq_count, ZN * share, wide)
    half = wide // 2
    seq_grads = jnp.einsum(
        "slk,slm->skm", low[:, :, :half], low[:, :, half:], precision=lax.Precision.HIGHEST
    ).reshape(seq_count, half * half)
    first_seq = lax.axis_index("dp") * seq_count
    mine = lax.dynamic_slice_in_dim(assignment, first_seq, seq_count, 0)
    ids = jnp.arange(DP * EX_DEV, dtype=jnp.int32)
    one_hot = (ids[:, None] == mine[None, :]).astype(jnp.float32)
    sent = jnp.sum(one_hot[:, :, None] * seq_grads[None], 1)
    sent = sent.reshape(DP, EX_DEV, half * half)
    got = lax.all_to_all(sent, "dp", 0, 0, tiled=True)
    example_grads = jnp.sum(got, 0)
    example_grads = example_grads + move(example_grads, ACROSS)
    example_grads = example_grads + move(example_grads, CORE)
    scores = jnp.dot(example_grads, queries.astype(jnp.float32).T, precision=lax.Precision.HIGHEST)

    total = mul(own_col, weights(xh, z)) + mul(other_col, weights(1 - xh, z))
    for step in range(1, 4):
        own_col = move(own_col, ALONG)
        other_col = move(other_col, ALONG)
        own_swap = move(own_col, CORE)
        other_swap = move(other_col, CORE)
        total = total + mul(own_col, weights(xh, z - step * toward))
        total = total + mul(other_col, weights(1 - xh, z - step * toward))
        total = total + mul(own_swap, weights(xh, z + step * toward))
        total = total + mul(other_swap, weights(1 - xh, z + step * toward))
    own_half = move(lax.dynamic_slice_in_dim(own_col, core * width, width, 1), ALONG)
    other_half = move(lax.dynamic_slice_in_dim(other_col, core * width, width, 1), ALONG)
    own_col = both(own_half, move(own_half, CORE))
    other_col = both(other_half, move(other_half, CORE))
    total = total + mul(own_col, weights(xh, z + 4))
    total = total + mul(other_col, weights(1 - xh, z + 4))
    return (total.astype(jnp.bfloat16), scores)


def solution(mesh):
    placed = (
        P("dp", "tensor"),
        P("dp", "tensor"),
        P("tensor", None),
        P(None, "tensor"),
        P(None, "tensor"),
        P("tensor", None),
        P(),
    )
    return jax.shard_map(
        on_device,
        mesh=mesh,
        in_specs=placed,
        out_specs=(P("dp", "tensor"), P("dp", "tensor")),
        check_vma=False,
    )
```

time: 525 us -> 138 us (0.26); the launches traced: 518 us -> 137 us
  waiting for transfers between devices: 451 us -> 14.2 us
  starting transfers between devices: 0.11 us -> 66.8 us
  blocking collectives: 24.6 us -> 0 us
  matrix products: 27.9 us -> 48.2 us
  between operations: 13.8 us -> 0.86 us
    psum x1 -> x0, waiting for transfers between devices: 243 us -> none  [on_device(): act_low = lax.psum(act_part, 'tensor')]
    all_gather x2 -> x0, waiting for transfers between devices: 206 us -> none  [the longest x1 130 us: on_device(): grad_piece = lax.all_gather(out_grad, 'tensor', axis=1, tiled=True)]
    ppermute x0 -> x23, starting transfers between devices: none -> 52.1 us  [move(): return lax.ppermute(value, 'tensor', perm)]
    all_gather x1 -> x0, blocking collectives: 24.6 us -> none  [on_device(): all_grads = lax.all_gather(proj_grads, 'dp', axis=0, tiled=True)]
    dot_general x6 -> x20, matrix products: 27.9 us -> 48.2 us  [the longest x18 46.9 us: mul(): lax.dot_general(rows, weights, (((1,), (1,)), ((), ())), preferred_elemen...]
    all_to_all x0 -> x3, starting transfers between devices: none -> 14.7 us  [the longest x2 10.1 us: on_device(): lax.all_to_all(low, 'tensor', 0, 0, axis_index_groups=Z_GROUPS, tiled=True)]
    all_to_all x0 -> x3, waiting for transfers between devices: none -> 8.17 us  [the longest x2 5.46 us: on_device(): lax.all_to_all(low, 'tensor', 0, 0, axis_index_groups=Z_GROUPS, tiled=True)]
    ppermute x0 -> x23, waiting for transfers between devices: none -> 6.05 us  [move(): return lax.ppermute(value, 'tensor', perm)]
  transfers between devices with their start and end apart: 3 -> 26, of which waited for: 3 -> 6; matrix products, arithmetic and copies ran while one was open for 2% -> 29% of each run, Pallas kernels for 0% -> 0%
where the time goes in v1:
time: 138 us; the launch traced here: 137 us
  starting transfers between devices  66.8 us (48%)
  matrix products  48.2 us (35%)
  waiting for transfers between devices  14.2 us (10%)
  local copies, waits for them, and re-layouts  3.8 us (3%)
  other arithmetic  2.99 us (2%)
    ppermute x23, starting transfers between devices, move(): return lax.ppermute(value, 'tensor', perm)  52.1 us
    dot_general x18, matrix products, mul(): lax.dot_general(rows, weights, (((1,), (1,)), ((), ())), preferred_elemen...  46.9 us
    all_to_all x2, starting transfers between devices, on_device(): lax.all_to_all(low, 'tensor', 0, 0, axis_index_groups=Z_GROUPS, tiled=True)  10.1 us
    ppermute x23, waiting for transfers between devices, move(): return lax.ppermute(value, 'tensor', perm)  6.05 us
    all_to_all x2, waiting for transfers between devices, on_device(): lax.all_to_all(low, 'tensor', 0, 0, axis_index_groups=Z_GROUPS, tiled=True)  5.46 us
    all_to_all x1, starting transfers between devices, on_device(): got = lax.all_to_all(sent, 'dp', 0, 0, tiled=True)  4.62 us
  transfers between devices with their start and end apart: 26, of which 6 were waited for; matrix products, arithmetic and copies ran while one was open for 29% of the time, Pallas kernels for 0%

profile of v1, /device:TPU:1, one launch (start us, length us, event | category | flops | bytes accessed | tf_op | source)
XLA Modules:
  0.0 136.9 jit_solution(13645554826700046179)
XLA Ops:
  0.6 0.0 copy-start
  0.7 1.2 copy-done
  1.8 1.3 fusion.70
  3.2 1.3 fusion.71
  4.5 0.2 copy.21
  4.7 3.3 %collective-permute-start.19 = (f32[3,128,128]{2,1,0:T(8,128)S(1)}, f32[3,128,128]{2,1,0:T(8,128)S(1)}, u32[]{:S(2)}, u32[]{:S(2)}) collective-permute-start(f32[3,128,128]{2,1,0:T(8,128)S(1)} %constant_dynamic-slice_fusion.1), channel_id=1, source_target_pairs={{0,1},{1,0},{2,3},{3,2},{4,5},{5,4},{6,7},{7,6},{8,9},{9,8},{10,11... | collective-permute-start | bytes 589832 | tf_op jit(solution)/shard_map/ppermute | solution.py:33
  8.0 1.1 collective-permute-done.19
  9.2 1.1 collective-permute-start.20
  10.3 4.5 %collective-permute-done.20 = f32[3,64,128]{2,1,0:T(8,128)S(1)} collective-permute-done((f32[3,64,128]{2,1,0:T(8,128)S(1)}, f32[3,64,128]{2,1,0:T(8,128)S(1)}, u32[]{:S(2)}, u32[]{:S(2)}) %collective-permute-start.20) | collective-permute-done | bytes 98336 | tf_op jit(solution)/shard_map/ppermute | solution.py:33
  14.8 0.6 copy.22
  15.4 6.5 %all-to-all-start = ((f32[8,3,8,128]{3,2,1,0:T(8,128)}), f32[8,3,8,128]{3,2,1,0:T(8,128)S(1)}, u32[]{:S(2)}, u32[]{:S(2)}) async-start(f32[8,3,8,128]{3,2,1,0:T(8,128)} %copy.22), calls=%async_computation | async-start | bytes 196608 | tf_op jit(solution)/shard_map/all_to_all | solution.py:76
  21.9 1.6 %collective-permute-start = (bf16[768,256]{1,0:T(8,128)(2,1)S(1)}, bf16[768,256]{1,0:T(8,128)(2,1)S(1)}, u32[]{:S(2)}, u32[]{:S(2)}) collective-permute-start(bf16[768,256]{1,0:T(8,128)(2,1)S(1)} %copy-done.2), channel_id=1, source_target_pairs={{0,1},{1,0},{2,3},{3,2},{4,5},{5,4},{6,7},{7,6},{8,9},{9,8},{10,11... | collective-permute-start | bytes 1179656 | tf_op jit(solution)/shard_map/ppermute | solution.py:33
  23.4 2.8 %collective-permute-start.1 = (bf16[768,256]{1,0:T(8,128)(2,1)S(1)}, bf16[768,256]{1,0:T(8,128)(2,1)}, u32[]{:S(2)}, u32[]{:S(2)}) collective-permute-start(bf16[768,256]{1,0:T(8,128)(2,1)S(1)} %copy-done.2), channel_id=1, source_target_pairs={{0,16},{1,17},{2,18},{3,19},{4,20},{5,21},{6,22},{7,23},{8,24},{9,... | collective-permute-start | bytes 1179656 | tf_op jit(solution)/shard_map/ppermute | solution.py:33
  26.2 0.1 dynamic_slice.87
  26.3 3.2 %all-to-all-done = f32[8,3,8,128]{3,2,1,0:T(8,128)S(1)} async-done(((f32[8,3,8,128]{3,2,1,0:T(8,128)}), f32[8,3,8,128]{3,2,1,0:T(8,128)S(1)}, u32[]{:S(2)}, u32[]{:S(2)}) %all-to-all-start) | async-done | bytes 98336 | tf_op jit(solution)/shard_map/all_to_all | solution.py:76
  29.5 0.6 broadcast_in_dim.2
  30.1 3.7 %all-to-all-start.1 = ((f32[8,3,8,128]{3,2,1,0:T(8,128)}), f32[8,3,8,128]{3,2,1,0:T(8,128)S(1)}, u32[]{:S(2)}, u32[]{:S(2)}) async-start(f32[8,3,8,128]{3,2,1,0:T(8,128)} %broadcast_in_dim.2), calls=%async_computation.1 | async-start | bytes 196608 | tf_op jit(solution)/shard_map/all_to_all | solution.py:79
  33.8 0.1 fusion.67
  33.9 1.1 maximum_select_fusion
  34.9 2.7 %collective-permute-start.3 = (bf16[768,512]{1,0:T(8,128)(2,1)}, bf16[768,512]{1,0:T(8,128)(2,1)}, u32[]{:S(2)}, u32[]{:S(2)}) collective-permute-start(bf16[768,512]{1,0:T(8,128)(2,1)} %maximum_select_fusion), channel_id=1, source_target_pairs={{0,2},{1,15},{2,4},{3,1},{4,6},{5,3},{6,8},{7,5},{8,10},{9,7},{10,... | collective-permute-start | bytes 2359304 | tf_op jit(solution)/shard_map/ppermute | solution.py:33
  37.6 1.6 %collective-permute-start.2 = (bf16[768,256]{1,0:T(8,128)(2,1)}, bf16[768,256]{1,0:T(8,128)(2,1)}, u32[]{:S(2)}, u32[]{:S(2)}) collective-permute-start(bf16[768,256]{1,0:T(8,128)(2,1)} %collective-permute-done.1), channel_id=1, source_target_pairs={{0,1},{1,0},{2,3},{3,2},{4,5},{5,4},{6,7},{7,6},{8,9},{9,8},{10,11... | collective-permute-start | bytes 1179656 | tf_op jit(solution)/shard_map/ppermute | solution.py:33
  39.2 2.3 %all-to-all-done.1 = f32[8,3,8,128]{3,2,1,0:T(8,128)S(1)} async-done(((f32[8,3,8,128]{3,2,1,0:T(8,128)}), f32[8,3,8,128]{3,2,1,0:T(8,128)S(1)}, u32[]{:S(2)}, u32[]{:S(2)}) %all-to-all-start.1) | async-done | bytes 98336 | tf_op jit(solution)/shard_map/all_to_all | solution.py:79
  41.5 0.4 fusion.46
  41.9 0.1 mul.161
  42.0 0.1 multiply_reduce_fusion
  42.1 0.9 reshape.40
  42.9 4.6 %all-to-all-start.2 = ((f32[8,2,4096]{2,1,0:T(2,128)}), f32[8,2,4096]{2,1,0:T(2,128)S(1)}, u32[]{:S(2)}, u32[]{:S(2)}) async-start(f32[8,2,4096]{2,1,0:T(2,128)} %reshape.40), calls=%async_computation.2 | async-start | bytes 524288 | tf_op jit(solution)/shard_map/all_to_all | solution.py:91
  47.6 3.4 %fusion.44 = f32[768,640]{1,0:T(8,128)} fusion(bf16[768,512]{1,0:T(8,128)(2,1)} %maximum_select_fusion, bf16[640,8192]{1,0:T(8,128)(2,1)} %param.9, s32[]{:T(128)S(6)} %select_n.89), kind=kOutput, calls=%fused_computation.48 | convolution fusion | flops 503316480 | bytes 3407876 | tf_op jit(solution)/shard_map/dot_general | solution.py:37
  51.0 2.7 %all-to-all-done.2 = f32[8,2,4096]{2,1,0:T(2,128)S(1)} async-done(((f32[8,2,4096]{2,1,0:T(2,128)}), f32[8,2,4096]{2,1,0:T(2,128)S(1)}, u32[]{:S(2)}, u32[]{:S(2)}) %all-to-all-start.2) | async-done | bytes 262176 | tf_op jit(solution)/shard_map/all_to_all | solution.py:91
  53.7 0.1 reduce_sum.29
  53.8 2.5 %collective-permute-start.21 = (f32[2,4096]{1,0:T(2,128)S(1)}, f32[2,4096]{1,0:T(2,128)S(1)}, u32[]{:S(2)}, u32[]{:S(2)}) collective-permute-start(f32[2,4096]{1,0:T(2,128)S(1)} %reduce_sum.29), channel_id=1, source_target_pairs={{0,16},{1,17},{2,18},{3,19},{4,20},{5,21},{6,22},{7,23},{8,24},{9,... | collective-permute-start | bytes 98312 | tf_op jit(solution)/shard_map/ppermute | solution.py:33
  56.3 1.5 %maximum_select_fusion.1 = bf16[768,512]{1,0:T(8,128)(2,1)S(1)} fusion(bf16[768,256]{1,0:T(8,128)(2,1)} %collective-permute-done.2, bf16[768,256]{1,0:T(8,128)(2,1)} %collective-permute-done.1, pred[]{:T(512)S(6)} %eq.23), kind=kLoop, calls=%fused_computation.2 | loop fusion | flops 3538944 | bytes 1572865 | tf_op jit(solution)/shard_map/jit(_where)/select_n | solution.py:53
  57.9 0.1 collective-permute-start.4
  58.0 0.4 collective-permute-done.21
  58.4 6.7 %collective-permute-start.22 = (f32[2,4096]{1,0:T(2,128)S(1)}, f32[2,4096]{1,0:T(2,128)S(1)}, u32[]{:S(2)}, u32[]{:S(2)}) collective-permute-start(f32[2,4096]{1,0:T(2,128)S(1)} %add.286), channel_id=1, source_target_pairs={{0,1},{1,0},{2,3},{3,2},{4,5},{5,4},{6,7},{7,6},{8,9},{9,8},{10,11... | collective-permute-start | bytes 98312 | tf_op jit(solution)/shard_map/ppermute | solution.py:33
  65.1 1.9 %fusion.42 = f32[768,640]{1,0:T(8,128)S(1)} fusion(bf16[768,512]{1,0:T(8,128)(2,1)S(1)} %maximum_select_fusion.1, bf16[640,8192]{1,0:T(8,128)(2,1)} %param.9, s32[]{:T(128)S(6)} %select_n.91), kind=kOutput, calls=%fused_computation.46 | convolution fusion | flops 503316480 | bytes 3407876 | tf_op jit(solution)/shard_map/dot_general | solution.py:37
  67.0 2.0 %collective-permute-start.7 = (bf16[768,512]{1,0:T(8,128)(2,1)}, bf16[768,512]{1,0:T(8,128)(2,1)S(1)}, u32[]{:S(2)}, u32[]{:S(2)}) collective-permute-start(bf16[768,512]{1,0:T(8,128)(2,1)} %collective-permute-done.3), channel_id=1, source_target_pairs={{0,2},{1,15},{2,4},{3,1},{4,6},{5,3},{6,8},{7,5},{8,10},{9,7},{10,... | collective-permute-start | bytes 2359304 | tf_op jit(solution)/shard_map/ppermute | solution.py:33
  69.0 0.9 fusion.49
  69.9 2.3 %fusion.40 = f32[768,640]{1,0:T(8,128)S(1)} fusion(bf16[768,512]{1,0:T(8,128)(2,1)} %collective-permute-done.3, bf16[640,8192]{1,0:T(8,128)(2,1)} %param.9, s32[]{:T(128)S(6)} %select_n.92), kind=kOutput, calls=%fused_computation.44 | convolution fusion | flops 503316480 | bytes 3407876 | tf_op jit(solution)/shard_map/dot_general | solution.py:37
  72.2 1.2 collective-permute-start.8
  73.4 3.7 %collective-permute-start.6 = (bf16[768,512]{1,0:T(8,128)(2,1)S(1)}, bf16[768,512]{1,0:T(8,128)(2,1)S(1)}, u32[]{:S(2)}, u32[]{:S(2)}) collective-permute-start(bf16[768,512]{1,0:T(8,128)(2,1)S(1)} %collective-permute-done.4), channel_id=1, source_target_pairs={{0,1},{1,0},{2,3},{3,2},{4,5},{5,4},{6,7},{7,6},{8,9},{9,8},{10,11... | collective-permute-start | bytes 2359304 | tf_op jit(solution)/shard_map/ppermute | solution.py:33
  77.2 1.9 %fusion.38 = f32[768,640]{1,0:T(8,128)S(1)} fusion(bf16[768,512]{1,0:T(8,128)(2,1)S(1)} %collective-permute-done.4, bf16[640,8192]{1,0:T(8,128)(2,1)} %param.9, s32[]{:T(128)S(6)} %select_n.93), kind=kOutput, calls=%fused_computation.42 | convolution fusion | flops 503316480 | bytes 3407876 | tf_op jit(solution)/shard_map/dot_general | solution.py:37
  79.1 3.0 %collective-permute-start.11 = (bf16[768,512]{1,0:T(8,128)(2,1)S(1)}, bf16[768,512]{1,0:T(8,128)(2,1)S(1)}, u32[]{:S(2)}, u32[]{:S(2)}) collective-permute-start(bf16[768,512]{1,0:T(8,128)(2,1)S(1)} %collective-permute-done.7), channel_id=1, source_target_pairs={{0,2},{1,15},{2,4},{3,1},{4,6},{5,3},{6,8},{7,5},{8,10},{9,7},{10,... | collective-permute-start | bytes 2359304 | tf_op jit(solution)/shard_map/ppermute | solution.py:33
  82.1 3.5 %collective-permute-start.9 = (bf16[768,512]{1,0:T(8,128)(2,1)S(1)}, bf16[768,512]{1,0:T(8,128)(2,1)S(1)}, u32[]{:S(2)}, u32[]{:S(2)}) collective-permute-start(bf16[768,512]{1,0:T(8,128)(2,1)S(1)} %collective-permute-done.7), channel_id=1, source_target_pairs={{0,1},{1,0},{2,3},{3,2},{4,5},{5,4},{6,7},{7,6},{8,9},{9,8},{10,11... | collective-permute-start | bytes 2359304 | tf_op jit(solution)/shard_map/ppermute | solution.py:33
  85.6 3.2 %fusion.32 = f32[768,640]{1,0:T(8,128)} fusion(bf16[768,512]{1,0:T(8,128)(2,1)S(1)} %collective-permute-done.7, bf16[640,8192]{1,0:T(8,128)(2,1)} %param.9, s32[]{:T(128)S(6)} %select_n.96), kind=kOutput, calls=%fused_computation.36 | convolution fusion | flops 503316480 | bytes 3407876 | tf_op jit(solution)/shard_map/dot_general | solution.py:37
  88.8 2.1 %fusion.36 = f32[768,640]{1,0:T(8,128)} fusion(bf16[768,512]{1,0:T(8,128)(2,1)S(1)} %collective-permute-done.5, bf16[640,8192]{1,0:T(8,128)(2,1)S(1)} %bitcast.30, s32[]{:T(128)S(6)} %select_n.94), kind=kOutput, calls=%fused_computation.40 | convolution fusion | flops 503316480 | bytes 3407876 | tf_op jit(solution)/shard_map/dot_general | solution.py:37
  90.9 3.0 %collective-permute-start.12 = (bf16[768,512]{1,0:T(8,128)(2,1)S(1)}, bf16[768,512]{1,0:T(8,128)(2,1)S(1)}, u32[]{:S(2)}, u32[]{:S(2)}) collective-permute-start(bf16[768,512]{1,0:T(8,128)(2,1)S(1)} %collective-permute-done.8), channel_id=1, source_target_pairs={{0,2},{1,15},{2,4},{3,1},{4,6},{5,3},{6,8},{7,5},{8,10},{9,7},{10,... | collective-permute-start | bytes 2359304 | tf_op jit(solution)/shard_map/ppermute | solution.py:33
  93.9 0.1 collective-permute-start.10
  94.0 2.1 %fusion.30 = f32[768,640]{1,0:T(8,128)} fusion(bf16[768,512]{1,0:T(8,128)(2,1)S(1)} %collective-permute-done.8, bf16[640,8192]{1,0:T(8,128)(2,1)S(1)} %bitcast.30, s32[]{:T(128)S(6)} %select_n.97), kind=kOutput, calls=%fused_computation.34 | convolution fusion | flops 503316480 | bytes 3407876 | tf_op jit(solution)/shard_map/dot_general | solution.py:37
  96.1 2.1 %fusion.34 = f32[768,640]{1,0:T(8,128)} fusion(bf16[768,512]{1,0:T(8,128)(2,1)S(1)} %collective-permute-done.6, bf16[640,8192]{1,0:T(8,128)(2,1)S(1)} %bitcast.30, s32[]{:T(128)S(6)} %select_n.95), kind=kOutput, calls=%fused_computation.38 | convolution fusion | flops 503316480 | bytes 3407876 | tf_op jit(solution)/shard_map/dot_general | solution.py:37
  98.3 3.0 %collective-permute-start.15 = (bf16[768,256]{1,0:T(8,128)(2,1)S(1)}, bf16[768,256]{1,0:T(8,128)(2,1)S(1)}, u32[]{:S(2)}, u32[]{:S(2)}) collective-permute-start(bf16[768,256]{1,0:T(8,128)(2,1)S(1)} %constant_dynamic-slice_fusion.3), channel_id=1, source_target_pairs={{0,2},{1,15},{2,4},{3,1},{4,6},{5,3},{6,8},{7,5},{8,10},{9,7},{10,... | collective-permute-start | bytes 1179656 | tf_op jit(solution)/shard_map/ppermute | solution.py:33
  101.3 1.4 %collective-permute-start.13 = (bf16[768,512]{1,0:T(8,128)(2,1)S(1)}, bf16[768,512]{1,0:T(8,128)(2,1)S(1)}, u32[]{:S(2)}, u32[]{:S(2)}) collective-permute-start(bf16[768,512]{1,0:T(8,128)(2,1)S(1)} %collective-permute-done.11), channel_id=1, source_target_pairs={{0,1},{1,0},{2,3},{3,2},{4,5},{5,4},{6,7},{7,6},{8,9},{9,8},{10,11... | collective-permute-start | bytes 2359304 | tf_op jit(solution)/shard_map/ppermute | solution.py:33
  102.7 2.1 %fusion.24 = f32[768,640]{1,0:T(8,128)} fusion(bf16[768,512]{1,0:T(8,128)(2,1)S(1)} %collective-permute-done.11, bf16[640,8192]{1,0:T(8,128)(2,1)S(1)} %bitcast.30, s32[]{:T(128)S(6)} %select_n.100), kind=kOutput, calls=%fused_computation.28 | convolution fusion | flops 503316480 | bytes 3407876 | tf_op jit(solution)/shard_map/dot_general | solution.py:37
  104.8 2.1 %fusion.28 = f32[768,640]{1,0:T(8,128)} fusion(bf16[768,512]{1,0:T(8,128)(2,1)S(1)} %collective-permute-done.9, bf16[640,8192]{1,0:T(8,128)(2,1)S(1)} %bitcast.30, s32[]{:T(128)S(6)} %select_n.98), kind=kOutput, calls=%fused_computation.32 | convolution fusion | flops 503316480 | bytes 3407876 | tf_op jit(solution)/shard_map/dot_general | solution.py:37
  106.9 2.9 %collective-permute-start.17 = (bf16[768,256]{1,0:T(8,128)(2,1)S(1)}, bf16[768,256]{1,0:T(8,128)(2,1)S(1)}, u32[]{:S(2)}, u32[]{:S(2)}) collective-permute-start(bf16[768,256]{1,0:T(8,128)(2,1)S(1)} %constant_dynamic-slice_fusion.2), channel_id=1, source_target_pairs={{0,2},{1,15},{2,4},{3,1},{4,6},{5,3},{6,8},{7,5},{8,10},{9,7},{10,... | collective-permute-start | bytes 1179656 | tf_op jit(solution)/shard_map/ppermute | solution.py:33
  109.9 1.2 collective-permute-start.14
  111.1 4.0 %collective-permute-start.16 = (bf16[768,256]{1,0:T(8,128)(2,1)S(1)}, bf16[768,256]{1,0:T(8,128)(2,1)S(1)}, u32[]{:S(2)}, u32[]{:S(2)}) collective-permute-start(bf16[768,256]{1,0:T(8,128)(2,1)S(1)} %collective-permute-done.15), channel_id=1, source_target_pairs={{0,1},{1,0},{2,3},{3,2},{4,5},{5,4},{6,7},{7,6},{8,9},{9,8},{10,11... | collective-permute-start | bytes 1179656 | tf_op jit(solution)/shard_map/ppermute | solution.py:33
  115.1 2.1 %fusion.22 = f32[768,640]{1,0:T(8,128)} fusion(bf16[768,512]{1,0:T(8,128)(2,1)S(1)} %collective-permute-done.12, bf16[640,8192]{1,0:T(8,128)(2,1)S(1)} %bitcast.30, s32[]{:T(128)S(6)} %select_n.101), kind=kOutput, calls=%fused_computation.26 | convolution fusion | flops 503316480 | bytes 3407876 | tf_op jit(solution)/shard_map/dot_general | solution.py:37
  117.2 2.1 %fusion.26 = f32[768,640]{1,0:T(8,128)} fusion(bf16[768,512]{1,0:T(8,128)(2,1)S(1)} %collective-permute-done.10, bf16[640,8192]{1,0:T(8,128)(2,1)S(1)} %bitcast.30, s32[]{:T(128)S(6)} %select_n.99), kind=kOutput, calls=%fused_computation.30 | convolution fusion | flops 503316480 | bytes 3407876 | tf_op jit(solution)/shard_map/dot_general | solution.py:37
  119.3 0.7 collective-permute-start.18
  120.0 2.1 %fusion = f32[768,640]{1,0:T(8,128)} fusion(bf16[768,256]{1,0:T(8,128)(2,1)S(1)} %collective-permute-done.16, bf16[768,256]{1,0:T(8,128)(2,1)S(1)} %collective-permute-done.15, pred[]{:T(512)S(6)} %eq.23, bf16[640,8192]{1,0:T(8,128)(2,1)S(1)} %bitcast.30, s32[]{:T(128)S(6)} %select_n.106), kind=kOutput, calls=%fused_computation.4 | convolution fusion | flops 506855424 | bytes 3407877 | tf_op jit(solution)/shard_map/dot_general | solution.py:37
  122.1 2.2 %fusion.20 = f32[768,640]{1,0:T(8,128)} fusion(bf16[768,512]{1,0:T(8,128)(2,1)S(1)} %collective-permute-done.13, bf16[640,8192]{1,0:T(8,128)(2,1)S(1)} %bitcast.30, s32[]{:T(128)S(6)} %select_n.102), kind=kOutput, calls=%fused_computation.24 | convolution fusion | flops 503316480 | bytes 3407876 | tf_op jit(solution)/shard_map/dot_general | solution.py:37
  124.3 2.1 %fusion.6 = f32[768,640]{1,0:T(8,128)} fusion(bf16[768,256]{1,0:T(8,128)(2,1)S(1)} %collective-permute-done.18, bf16[768,256]{1,0:T(8,128)(2,1)S(1)} %collective-permute-done.17, pred[]{:T(512)S(6)} %eq.23, bf16[640,8192]{1,0:T(8,128)(2,1)S(1)} %bitcast.30, s32[]{:T(128)S(6)} %select_n.108), kind=kOutput, calls=%fused_computation.11 | convolution fusion | flops 506855424 | bytes 3407877 | tf_op jit(solution)/shard_map/dot_general | solution.py:37
  126.4 10.5 %add_convert_fusion = bf16[768,640]{1,0:T(8,128)(2,1)} fusion(f32[768,640]{1,0:T(8,128)} %fusion.6, f32[768,640]{1,0:T(8,128)} %fusion, f32[768,640]{1,0:T(8,128)} %fusion.20, f32[768,640]{1,0:T(8,128)} %fusion.22, f32[768,640]{1,0:T(8,128)} %fusion.24, f32[768,640]{1,0:T(8,128)} %fusion.26, f32[768,640]{1,0:T(8,128)} %fusion.28, f32[768,640]{1,0:T(8,128)} %fusion.30, ...), kind=kOutput, calls=%fused_computation | convolution fusion | flops 511180800 | bytes 31916036 | tf_op jit(solution)/shard_map/dot_general | solution.py:37
  (46 shorter events, 0.3 us)
Async XLA Ops:
  0.6 1.2 copy-start
  3.1 18.7 %copy-start.2 = (bf16[768,256]{1,0:T(8,128)(2,1)S(1)}, bf16[768,256]{1,0:T(8,128)(2,1)}, u32[]{:S(2)}) copy-start(bf16[768,256]{1,0:T(8,128)(2,1)} %param.8) | copy-start | bytes 1179652
  3.1 23.1 %copy-start.4 = (s32[24]{0:T(128)S(1)}, s32[24]{0:T(128)}, u32[]{:S(2)}) copy-start(s32[24]{0:T(128)} %param.13) | copy-start | bytes 292
  4.7 4.4 %collective-permute-start.19 = (f32[3,128,128]{2,1,0:T(8,128)S(1)}, f32[3,128,128]{2,1,0:T(8,128)S(1)}, u32[]{:S(2)}, u32[]{:S(2)}) collective-permute-start(f32[3,128,128]{2,1,0:T(8,128)S(1)} %constant_dynamic-slice_fusion.1), channel_id=1, source_target_pairs={{0,1},{1,0},{2,3},{3,2},{4,5},{5,4},{6,7},{7,6},{8,9},{9,8},{10,11... | collective-permute-start | bytes 589832 | tf_op jit(solution)/shard_map/ppermute | solution.py:33
  9.2 5.6 %collective-permute-start.20 = (f32[3,64,128]{2,1,0:T(8,128)S(1)}, f32[3,64,128]{2,1,0:T(8,128)S(1)}, u32[]{:S(2)}, u32[]{:S(2)}) collective-permute-start(f32[3,64,128]{2,1,0:T(8,128)S(1)} %constant_dynamic-slice_fusion), channel_id=1, source_target_pairs={{0,16},{1,17},{2,18},{3,19},{4,20},{5,21},{6,22},{7,23},{8,24},{9,... | collective-permute-start | bytes 294920 | tf_op jit(solution)/shard_map/ppermute | solution.py:33
  15.4 14.0 %all-to-all-start = ((f32[8,3,8,128]{3,2,1,0:T(8,128)}), f32[8,3,8,128]{3,2,1,0:T(8,128)S(1)}, u32[]{:S(2)}, u32[]{:S(2)}) async-start(f32[8,3,8,128]{3,2,1,0:T(8,128)} %copy.22), calls=%async_computation | async-start | bytes 196608 | tf_op jit(solution)/shard_map/all_to_all | solution.py:76
  21.9 12.0 %collective-permute-start = (bf16[768,256]{1,0:T(8,128)(2,1)S(1)}, bf16[768,256]{1,0:T(8,128)(2,1)S(1)}, u32[]{:S(2)}, u32[]{:S(2)}) collective-permute-start(bf16[768,256]{1,0:T(8,128)(2,1)S(1)} %copy-done.2), channel_id=1, source_target_pairs={{0,1},{1,0},{2,3},{3,2},{4,5},{5,4},{6,7},{7,6},{8,9},{9,8},{10,11... | collective-permute-start | bytes 1179656 | tf_op jit(solution)/shard_map/ppermute | solution.py:33
  23.4 14.1 %collective-permute-start.1 = (bf16[768,256]{1,0:T(8,128)(2,1)S(1)}, bf16[768,256]{1,0:T(8,128)(2,1)}, u32[]{:S(2)}, u32[]{:S(2)}) collective-permute-start(bf16[768,256]{1,0:T(8,128)(2,1)S(1)} %copy-done.2), channel_id=1, source_target_pairs={{0,16},{1,17},{2,18},{3,19},{4,20},{5,21},{6,22},{7,23},{8,24},{9,... | collective-permute-start | bytes 1179656 | tf_op jit(solution)/shard_map/ppermute | solution.py:33
  30.1 11.4 %all-to-all-start.1 = ((f32[8,3,8,128]{3,2,1,0:T(8,128)}), f32[8,3,8,128]{3,2,1,0:T(8,128)S(1)}, u32[]{:S(2)}, u32[]{:S(2)}) async-start(f32[8,3,8,128]{3,2,1,0:T(8,128)} %broadcast_in_dim.2), calls=%async_computation.1 | async-start | bytes 196608 | tf_op jit(solution)/shard_map/all_to_all | solution.py:79
  34.9 32.1 %collective-permute-start.3 = (bf16[768,512]{1,0:T(8,128)(2,1)}, bf16[768,512]{1,0:T(8,128)(2,1)}, u32[]{:S(2)}, u32[]{:S(2)}) collective-permute-start(bf16[768,512]{1,0:T(8,128)(2,1)} %maximum_select_fusion), channel_id=1, source_target_pairs={{0,2},{1,15},{2,4},{3,1},{4,6},{5,3},{6,8},{7,5},{8,10},{9,7},{10,... | collective-permute-start | bytes 2359304 | tf_op jit(solution)/shard_map/ppermute | solution.py:33
  37.6 18.8 %collective-permute-start.2 = (bf16[768,256]{1,0:T(8,128)(2,1)}, bf16[768,256]{1,0:T(8,128)(2,1)}, u32[]{:S(2)}, u32[]{:S(2)}) collective-permute-start(bf16[768,256]{1,0:T(8,128)(2,1)} %collective-permute-done.1), channel_id=1, source_target_pairs={{0,1},{1,0},{2,3},{3,2},{4,5},{5,4},{6,7},{7,6},{8,9},{9,8},{10,11... | collective-permute-start | bytes 1179656 | tf_op jit(solution)/shard_map/ppermute | solution.py:33
  41.5 47.3 %slice-start = ((s8[10485760]{0:T(1024)(128)(4,1)}), s8[2097152]{0:T(1024)(128)(4,1)S(1)}, s32[]{:S(2)}) async-start(s8[10485760]{0:T(1024)(128)(4,1)} %bitcast.29), calls=%async_computation.3 | async-start | bytes 4194304
  42.9 10.7 %all-to-all-start.2 = ((f32[8,2,4096]{2,1,0:T(2,128)}), f32[8,2,4096]{2,1,0:T(2,128)S(1)}, u32[]{:S(2)}, u32[]{:S(2)}) async-start(f32[8,2,4096]{2,1,0:T(2,128)} %reshape.40), calls=%async_computation.2 | async-start | bytes 524288 | tf_op jit(solution)/shard_map/all_to_all | solution.py:91
  53.8 35.0 %slice-start.1 = ((s8[10485760]{0:T(1024)(128)(4,1)}), s8[4194304]{0:T(1024)(128)(4,1)S(1)}, s32[]{:S(2)}) async-start(s8[10485760]{0:T(1024)(128)(4,1)} %bitcast.29), calls=%async_computation.4 | async-start | bytes 8388608
  53.8 4.6 %collective-permute-start.21 = (f32[2,4096]{1,0:T(2,128)S(1)}, f32[2,4096]{1,0:T(2,128)S(1)}, u32[]{:S(2)}, u32[]{:S(2)}) collective-permute-start(f32[2,4096]{1,0:T(2,128)S(1)} %reduce_sum.29), channel_id=1, source_target_pairs={{0,16},{1,17},{2,18},{3,19},{4,20},{5,21},{6,22},{7,23},{8,24},{9,... | collective-permute-start | bytes 98312 | tf_op jit(solution)/shard_map/ppermute | solution.py:33
  57.9 11.1 %copy-start.3 = (bf16[32,4096]{1,0:T(8,128)(2,1)S(1)}, bf16[32,4096]{1,0:T(8,128)(2,1)}, u32[]{:S(2)}) copy-start(bf16[32,4096]{1,0:T(8,128)(2,1)} %param.12) | copy-start | bytes 786436
  57.9 14.3 %collective-permute-start.4 = (bf16[768,512]{1,0:T(8,128)(2,1)S(1)}, bf16[768,512]{1,0:T(8,128)(2,1)S(1)}, u32[]{:S(2)}, u32[]{:S(2)}) collective-permute-start(bf16[768,512]{1,0:T(8,128)(2,1)S(1)} %maximum_select_fusion.1), channel_id=1, source_target_pairs={{0,2},{1,15},{2,4},{3,1},{4,6},{5,3},{6,8},{7,5},{8,10},{9,7},{10,... | collective-permute-start | bytes 2359304 | tf_op jit(solution)/shard_map/ppermute | solution.py:33
  58.4 10.6 %collective-permute-start.22 = (f32[2,4096]{1,0:T(2,128)S(1)}, f32[2,4096]{1,0:T(2,128)S(1)}, u32[]{:S(2)}, u32[]{:S(2)}) collective-permute-start(f32[2,4096]{1,0:T(2,128)S(1)} %add.286), channel_id=1, source_target_pairs={{0,1},{1,0},{2,3},{3,2},{4,5},{5,4},{6,7},{7,6},{8,9},{9,8},{10,11... | collective-permute-start | bytes 98312 | tf_op jit(solution)/shard_map/ppermute | solution.py:33
  67.0 12.1 %collective-permute-start.7 = (bf16[768,512]{1,0:T(8,128)(2,1)}, bf16[768,512]{1,0:T(8,128)(2,1)S(1)}, u32[]{:S(2)}, u32[]{:S(2)}) collective-permute-start(bf16[768,512]{1,0:T(8,128)(2,1)} %collective-permute-done.3), channel_id=1, source_target_pairs={{0,2},{1,15},{2,4},{3,1},{4,6},{5,3},{6,8},{7,5},{8,10},{9,7},{10,... | collective-permute-start | bytes 2359304 | tf_op jit(solution)/shard_map/ppermute | solution.py:33
  69.9 18.9 %slice-start.2 = ((s8[10485760]{0:T(1024)(128)(4,1)}), s8[4194304]{0:T(1024)(128)(4,1)S(1)}, s32[]{:S(2)}) async-start(s8[10485760]{0:T(1024)(128)(4,1)} %bitcast.29), calls=%async_computation.5 | async-start | bytes 8388608
  69.9 18.9 %collective-permute-start.5 = (bf16[768,512]{1,0:T(8,128)(2,1)}, bf16[768,512]{1,0:T(8,128)(2,1)S(1)}, u32[]{:S(2)}, u32[]{:S(2)}) collective-permute-start(bf16[768,512]{1,0:T(8,128)(2,1)} %collective-permute-done.3), channel_id=1, source_target_pairs={{0,1},{1,0},{2,3},{3,2},{4,5},{5,4},{6,7},{7,6},{8,9},{9,8},{10,11... | collective-permute-start | bytes 2359304 | tf_op jit(solution)/shard_map/ppermute | solution.py:33
  72.2 18.7 %collective-permute-start.8 = (bf16[768,512]{1,0:T(8,128)(2,1)S(1)}, bf16[768,512]{1,0:T(8,128)(2,1)S(1)}, u32[]{:S(2)}, u32[]{:S(2)}) collective-permute-start(bf16[768,512]{1,0:T(8,128)(2,1)S(1)} %collective-permute-done.4), channel_id=1, source_target_pairs={{0,2},{1,15},{2,4},{3,1},{4,6},{5,3},{6,8},{7,5},{8,10},{9,7},{10,... | collective-permute-start | bytes 2359304 | tf_op jit(solution)/shard_map/ppermute | solution.py:33
  73.4 22.7 %collective-permute-start.6 = (bf16[768,512]{1,0:T(8,128)(2,1)S(1)}, bf16[768,512]{1,0:T(8,128)(2,1)S(1)}, u32[]{:S(2)}, u32[]{:S(2)}) collective-permute-start(bf16[768,512]{1,0:T(8,128)(2,1)S(1)} %collective-permute-done.4), channel_id=1, source_target_pairs={{0,1},{1,0},{2,3},{3,2},{4,5},{5,4},{6,7},{7,6},{8,9},{9,8},{10,11... | collective-permute-start | bytes 2359304 | tf_op jit(solution)/shard_map/ppermute | solution.py:33
  79.1 19.1 %collective-permute-start.11 = (bf16[768,512]{1,0:T(8,128)(2,1)S(1)}, bf16[768,512]{1,0:T(8,128)(2,1)S(1)}, u32[]{:S(2)}, u32[]{:S(2)}) collective-permute-start(bf16[768,512]{1,0:T(8,128)(2,1)S(1)} %collective-permute-done.7), channel_id=1, source_target_pairs={{0,2},{1,15},{2,4},{3,1},{4,6},{5,3},{6,8},{7,5},{8,10},{9,7},{10,... | collective-permute-start | bytes 2359304 | tf_op jit(solution)/shard_map/ppermute | solution.py:33
  82.1 22.7 %collective-permute-start.9 = (bf16[768,512]{1,0:T(8,128)(2,1)S(1)}, bf16[768,512]{1,0:T(8,128)(2,1)S(1)}, u32[]{:S(2)}, u32[]{:S(2)}) collective-permute-start(bf16[768,512]{1,0:T(8,128)(2,1)S(1)} %collective-permute-done.7), channel_id=1, source_target_pairs={{0,1},{1,0},{2,3},{3,2},{4,5},{5,4},{6,7},{7,6},{8,9},{9,8},{10,11... | collective-permute-start | bytes 2359304 | tf_op jit(solution)/shard_map/ppermute | solution.py:33
  90.9 16.0 %collective-permute-start.12 = (bf16[768,512]{1,0:T(8,128)(2,1)S(1)}, bf16[768,512]{1,0:T(8,128)(2,1)S(1)}, u32[]{:S(2)}, u32[]{:S(2)}) collective-permute-start(bf16[768,512]{1,0:T(8,128)(2,1)S(1)} %collective-permute-done.8), channel_id=1, source_target_pairs={{0,2},{1,15},{2,4},{3,1},{4,6},{5,3},{6,8},{7,5},{8,10},{9,7},{10,... | collective-permute-start | bytes 2359304 | tf_op jit(solution)/shard_map/ppermute | solution.py:33
  93.9 23.3 %collective-permute-start.10 = (bf16[768,512]{1,0:T(8,128)(2,1)S(1)}, bf16[768,512]{1,0:T(8,128)(2,1)S(1)}, u32[]{:S(2)}, u32[]{:S(2)}) collective-permute-start(bf16[768,512]{1,0:T(8,128)(2,1)S(1)} %collective-permute-done.8), channel_id=1, source_target_pairs={{0,1},{1,0},{2,3},{3,2},{4,5},{5,4},{6,7},{7,6},{8,9},{9,8},{10,11... | collective-permute-start | bytes 2359304 | tf_op jit(solution)/shard_map/ppermute | solution.py:33
  98.3 12.8 %collective-permute-start.15 = (bf16[768,256]{1,0:T(8,128)(2,1)S(1)}, bf16[768,256]{1,0:T(8,128)(2,1)S(1)}, u32[]{:S(2)}, u32[]{:S(2)}) collective-permute-start(bf16[768,256]{1,0:T(8,128)(2,1)S(1)} %constant_dynamic-slice_fusion.3), channel_id=1, source_target_pairs={{0,2},{1,15},{2,4},{3,1},{4,6},{5,3},{6,8},{7,5},{8,10},{9,7},{10,... | collective-permute-start | bytes 1179656 | tf_op jit(solution)/shard_map/ppermute | solution.py:33
  101.3 20.8 %collective-permute-start.13 = (bf16[768,512]{1,0:T(8,128)(2,1)S(1)}, bf16[768,512]{1,0:T(8,128)(2,1)S(1)}, u32[]{:S(2)}, u32[]{:S(2)}) collective-permute-start(bf16[768,512]{1,0:T(8,128)(2,1)S(1)} %collective-permute-done.11), channel_id=1, source_target_pairs={{0,1},{1,0},{2,3},{3,2},{4,5},{5,4},{6,7},{7,6},{8,9},{9,8},{10,11... | collective-permute-start | bytes 2359304 | tf_op jit(solution)/shard_map/ppermute | solution.py:33
  106.9 12.3 %collective-permute-start.17 = (bf16[768,256]{1,0:T(8,128)(2,1)S(1)}, bf16[768,256]{1,0:T(8,128)(2,1)S(1)}, u32[]{:S(2)}, u32[]{:S(2)}) collective-permute-start(bf16[768,256]{1,0:T(8,128)(2,1)S(1)} %constant_dynamic-slice_fusion.2), channel_id=1, source_target_pairs={{0,2},{1,15},{2,4},{3,1},{4,6},{5,3},{6,8},{7,5},{8,10},{9,7},{10,... | collective-permute-start | bytes 1179656 | tf_op jit(solution)/shard_map/ppermute | solution.py:33
  109.9 16.5 %collective-permute-start.14 = (bf16[768,512]{1,0:T(8,128)(2,1)S(1)}, bf16[768,512]{1,0:T(8,128)(2,1)}, u32[]{:S(2)}, u32[]{:S(2)}) collective-permute-start(bf16[768,512]{1,0:T(8,128)(2,1)S(1)} %collective-permute-done.12), channel_id=1, source_target_pairs={{0,1},{1,0},{2,3},{3,2},{4,5},{5,4},{6,7},{7,6},{8,9},{9,8},{10,11... | collective-permute-start | bytes 2359304 | tf_op jit(solution)/shard_map/ppermute | solution.py:33
  111.1 8.9 %collective-permute-start.16 = (bf16[768,256]{1,0:T(8,128)(2,1)S(1)}, bf16[768,256]{1,0:T(8,128)(2,1)S(1)}, u32[]{:S(2)}, u32[]{:S(2)}) collective-permute-start(bf16[768,256]{1,0:T(8,128)(2,1)S(1)} %collective-permute-done.15), channel_id=1, source_target_pairs={{0,1},{1,0},{2,3},{3,2},{4,5},{5,4},{6,7},{7,6},{8,9},{9,8},{10,11... | collective-permute-start | bytes 1179656 | tf_op jit(solution)/shard_map/ppermute | solution.py:33
  119.3 5.0 %collective-permute-start.18 = (bf16[768,256]{1,0:T(8,128)(2,1)S(1)}, bf16[768,256]{1,0:T(8,128)(2,1)S(1)}, u32[]{:S(2)}, u32[]{:S(2)}) collective-permute-start(bf16[768,256]{1,0:T(8,128)(2,1)S(1)} %collective-permute-done.17), channel_id=1, source_target_pairs={{0,1},{1,0},{2,3},{3,2},{4,5},{5,4},{6,7},{7,6},{8,9},{9,8},{10,11... | collective-permute-start | bytes 1179656 | tf_op jit(solution)/shard_map/ppermute | solution.py:33
  124.3 2.1 %copy-start.1 = (f32[768,640]{1,0:T(8,128)S(1)}, f32[768,640]{1,0:T(8,128)}, u32[]{:S(2)}) copy-start(f32[768,640]{1,0:T(8,128)} %fusion.44) | copy-start | bytes 5898244

commit v2 on v1

v2 whole, which is shorter than its diff:
```python
import jax
import jax.numpy as jnp
from jax import lax
from jax.experimental import pallas as pl
from jax.experimental.pallas import tpu as pltpu
from jax.sharding import PartitionSpec as P

LEN = 256
EX_DEV = 2
DP = 8
TENSOR = 32
ZN = 8


def place(xh, z, c):
    return xh * 16 + (z % ZN) * 2 + c


def pairs(move):
    out = []
    for xh in range(2):
        for z in range(ZN):
            for c in range(2):
                out.append((place(xh, z, c), place(*move(xh, z, c))))
    return out


CORE = pairs(lambda xh, z, c: (xh, z, 1 - c))
ACROSS = pairs(lambda xh, z, c: (1 - xh, z, c))
ALONG = pairs(lambda xh, z, c: (xh, z + 1 - 2 * c, c))
Z_GROUPS = [[place(xh, z, c) for z in range(ZN)] for xh in range(2) for c in range(2)]


def move(value, perm):
    return lax.ppermute(value, "tensor", perm)


def mul(rows, weights):
    return lax.dot_general(rows, weights, (((1,), (1,)), ((), ())), preferred_element_type=jnp.float32)


def chunk_matmul(total, pieces, blocks, w_down, out_type):
    count = len(pieces)
    rows = pieces[0].shape[0]
    widths = [piece.shape[1] for piece in pieces]
    width = max(widths)
    unit = min(widths + [width // 2])
    outs = w_down.shape[0]
    tile = rows // 2
    started = total is not None

    def kernel(blocks_ref, *refs):
        piece_refs = refs[:count]
        w_ref = refs[count]
        total_ref = refs[count + 1] if started else None
        out_ref, x_buf, w_buf, sum_buf, old_buf, x_sem, w_sem, old_sem = refs[count + 1 + started:]
        x_copies = []
        w_copies = []
        for n in range(count):
            wide = widths[n]
            start = pl.multiple_of(blocks_ref[n] * unit, unit)
            x_copies.append(pltpu.make_async_copy(piece_refs[n], x_buf.at[n, :, pl.ds(0, wide)], x_sem.at[n]))
            w_copies.append(
                pltpu.make_async_copy(w_ref.at[:, pl.ds(start, wide)], w_buf.at[n, :, pl.ds(0, wide)], w_sem.at[n])
            )
        old_copy = pltpu.make_async_copy(total_ref, old_buf, old_sem) if started else None
        merge = min(1, count - 1)
        for n in range(count):
            w_copies[n].start()
            x_copies[n].start()
            if n == merge and started:
                old_copy.start()
        for n in range(count):
            x_copies[n].wait()
            w_copies[n].wait()
            last = n + 1 == count
            with_old = started and n == merge
            if with_old:
                old_copy.wait()

            def step(i, carry, n=n, last=last, with_old=with_old):
                at = pl.ds(pl.multiple_of(i * tile, tile), tile)
                part = mul(x_buf[n, at, pl.ds(0, widths[n])], w_buf[n, :, pl.ds(0, widths[n])])
                if n > 0:
                    part = part + sum_buf[at, :]
                if with_old:
                    part = part + old_buf[at, :]
                if last:
                    out_ref[at, :] = part.astype(out_type)
                else:
                    sum_buf[at, :] = part
                return carry

            lax.fori_loop(0, rows // tile, step, 0)

    anywhere = pl.BlockSpec(memory_space=pl.ANY)
    old = [total] if started else []
    return pl.pallas_call(
        kernel,
        out_shape=jax.ShapeDtypeStruct((rows, outs), out_type),
        in_specs=[pl.BlockSpec(memory_space=pltpu.SMEM)] + [anywhere] * (count + 1 + len(old)),
        out_specs=pl.BlockSpec(memory_space=pltpu.VMEM),
        scratch_shapes=[
            pltpu.VMEM((count, rows, width), jnp.bfloat16),
            pltpu.VMEM((count, outs, width), jnp.bfloat16),
            pltpu.VMEM((rows, outs), jnp.float32),
            pltpu.VMEM((rows, outs) if started else (8, 128), jnp.float32),
            pltpu.SemaphoreType.DMA((count,)),
            pltpu.SemaphoreType.DMA((count,)),
            pltpu.SemaphoreType.DMA,
        ],
        compiler_params=pltpu.CompilerParams(vmem_limit_bytes=60 << 20),
        cost_estimate=pl.CostEstimate(
            flops=2 * rows * outs * sum(widths),
            transcendentals=0,
            bytes_accessed=2 * sum(widths) * (rows + outs) + 8 * rows * outs,
        ),
        name="chunk_matmul",
    )(jnp.stack(blocks).astype(jnp.int32), *pieces, w_down, *old)


def on_device(hidden, out_grad, w_down, proj_in, proj_out, queries, assignment):
    rank = lax.axis_index("tensor")
    core = rank & 1
    z = (rank >> 1) & (ZN - 1)
    xh = rank >> 4
    toward = 1 - 2 * core
    width = out_grad.shape[1]

    def both(own, other):
        return jnp.where(core == 0, jnp.concatenate([own, other], 1), jnp.concatenate([other, own], 1))

    def halve(value, bit, perm):
        half = value.shape[1] // 2
        keep = lax.dynamic_slice_in_dim(value, bit * half, half, 1)
        give = lax.dynamic_slice_in_dim(value, (1 - bit) * half, half, 1)
        return keep + move(give, perm)

    together = lax.optimization_barrier
    pieces = []
    blocks = []

    def keep(column, depth, value):
        pieces.append(value)
        blocks.append(2 * (column * ZN + ((depth + 2 * ZN) & (ZN - 1))))

    def keep_half(column, value, side):
        pieces.append(value)
        blocks.append(2 * (column * ZN + ((z + 4) & (ZN - 1))) + side)

    def flush(total, out_type=jnp.float32):
        total = chunk_matmul(total, pieces, blocks, w_down, out_type)
        pieces.clear()
        blocks.clear()
        return total

    def mine_of(pair):
        return lax.dynamic_slice_in_dim(pair, core * width, width, 1)

    near, far = xh, 1 - xh
    other = move(out_grad, CORE)
    crossed = move(out_grad, ACROSS)
    other, hidden, proj_out = together((other, hidden, proj_out))
    own0 = both(out_grad, other)
    own1 = move(own0, ALONG)
    act_part = mul(hidden, proj_in)
    grad_part = mul(out_grad, proj_out)
    low = jnp.concatenate([act_part, grad_part], 1)
    seq_count = low.shape[0] // LEN
    wide = low.shape[1]
    low = low.reshape(seq_count, LEN, wide)
    low = halve(low, core, CORE)
    low = halve(low, xh, ACROSS)

    far0 = both(crossed, move(crossed, CORE))
    far1 = move(far0, ALONG)
    far0, low = together((far0, low))
    own2 = move(own1, ALONG)
    share = low.shape[1] // ZN
    low = low.reshape(seq_count, ZN, share, wide).transpose(1, 0, 2, 3)
    low = lax.all_to_all(low, "tensor", 0, 0, axis_index_groups=Z_GROUPS, tiled=True)
    low = jnp.sum(low, 0)

    swap1 = move(own1, CORE)
    own1, low = together((own1, low))
    far2 = move(far1, ALONG)
    swapf1 = move(far1, CORE)
    low = jnp.broadcast_to(low[None], (ZN,) + low.shape)
    low = lax.all_to_all(low, "tensor", 0, 0, axis_index_groups=Z_GROUPS, tiled=True)
    low = low.transpose(1, 0, 2, 3).reshape(seq_count, ZN * share, wide)
    half = wide // 2
    seq_grads = jnp.einsum(
        "slk,slm->skm", low[:, :, :half], low[:, :, half:], precision=lax.Precision.HIGHEST
    ).reshape(seq_count, half * half)
    first_seq = lax.axis_index("dp") * seq_count
    mine = lax.dynamic_slice_in_dim(assignment, first_seq, seq_count, 0)
    ids = jnp.arange(DP * EX_DEV, dtype=jnp.int32)
    one_hot = (ids[:, None] == mine[None, :]).astype(jnp.float32)
    sent = jnp.sum(one_hot[:, :, None] * seq_grads[None], 1)
    sent = sent.reshape(DP, EX_DEV, half * half)

    far1, sent = together((far1, sent))
    own3 = move(own2, ALONG)
    swap2 = move(own2, CORE)
    got = lax.all_to_all(sent, "dp", 0, 0, tiled=True)
    keep(near, z, own0)
    keep(far, z, far0)
    keep(near, z - toward, own1)
    keep(near, z + toward, swap1)
    keep(far, z - toward, far1)
    keep(far, z + toward, swapf1)
    total = flush(None)
    got, total = together((got, total))
    far3 = move(far2, ALONG)
    swapf2 = move(far2, CORE)
    example_grads = jnp.sum(got, 0)

    own2, example_grads = together((own2, example_grads))
    own4 = move(mine_of(own3), ALONG)
    swap3 = move(own3, CORE)
    example_grads = example_grads + move(example_grads, ACROSS)
    example_grads = example_grads + move(example_grads, CORE)
    scores = jnp.dot(example_grads, queries.astype(jnp.float32).T, precision=lax.Precision.HIGHEST)

    far2, scores = together((far2, scores))
    far4 = move(mine_of(far3), ALONG)
    swapf3 = move(far3, CORE)
    keep(near, z - 2 * toward, own2)
    keep(near, z + 2 * toward, swap2)
    keep(far, z - 2 * toward, far2)
    keep(far, z + 2 * toward, swapf2)
    keep(near, z - 3 * toward, own3)
    keep(near, z + 3 * toward, swap3)
    total = flush(total)
    far4, own4, total = together((far4, own4, total))
    swap4 = move(own4, CORE)
    swapf4 = move(far4, CORE)
    keep(far, z - 3 * toward, far3)
    keep(far, z + 3 * toward, swapf3)
    keep_half(near, own4, core)
    keep_half(near, swap4, 1 - core)
    keep_half(far, far4, core)
    keep_half(far, swapf4, 1 - core)
    total = flush(total, jnp.bfloat16)
    return (total, scores)


def solution(mesh):
    placed = (
        P("dp", "tensor"),
        P("dp", "tensor"),
        P("tensor", None),
        P(None, "tensor"),
        P(None, "tensor"),
        P("tensor", None),
        P(),
    )
    return jax.shard_map(
        on_device,
        mesh=mesh,
        in_specs=placed,
        out_specs=(P("dp", "tensor"), P("dp", "tensor")),
        check_vma=False,
    )
```

time: 138 us -> 121 us (0.88)
  matrix products: 48.2 us -> 2.89 us
  Pallas kernels: 0 us -> 29.1 us
  starting transfers between devices: 66.8 us -> 51.7 us
  waiting for transfers between devices: 14.2 us -> 27.1 us
  local copies, waits for them, and re-layouts: 3.8 us -> 6.87 us
    dot_general x18 -> x2, matrix products: 46.9 us -> 0.67 us  [mul(): lax.dot_general(rows, weights, (((1,), (1,)), ((), ())), preferred_elemen...]
    pallas_call x0 -> x3, Pallas kernels: none -> 29.1 us  [chunk_matmul(): pl.pallas_call(kernel, out_shape=jax.ShapeDtypeStruct((rows, outs), out_t...]
    ppermute x23, starting transfers between devices: 52.1 us -> 37 us  [move(): return lax.ppermute(value, 'tensor', perm)]
    all_to_all x2, waiting for transfers between devices: 5.46 us -> 14.2 us  [on_device(): lax.all_to_all(low, 'tensor', 0, 0, axis_index_groups=Z_GROUPS, tiled=True)]
    ppermute x23, waiting for transfers between devices: 6.05 us -> 12.9 us  [move(): return lax.ppermute(value, 'tensor', perm)]
    all_to_all x1, waiting for transfers between devices: 2.72 us -> 0.01 us  [on_device(): got = lax.all_to_all(sent, 'dp', 0, 0, tiled=True)]
    another operation x0 -> x3, local copies, waits for them, and re-layouts: none -> 1.85 us  [chunk_matmul(): jnp.stack(blocks).astype(jnp.int32)]
  transfers between devices with their start and end apart: 26 -> 26, of which waited for: 6 -> 10; matrix products, arithmetic and copies ran while one was open for 29% -> 8% of each run, Pallas kernels for 0% -> 17%
where the time goes in v2:
time: 121 us
  starting transfers between devices  51.7 us (43%)
  Pallas kernels  29.1 us (24%)
  waiting for transfers between devices  27.1 us (22%)
  local copies, waits for them, and re-layouts  6.87 us (6%)
  matrix products  2.89 us (2%)
  other arithmetic  1.88 us (2%)
    ppermute x23, starting transfers between devices, move(): return lax.ppermute(value, 'tensor', perm)  37 us
    pallas_call x3, Pallas kernels, chunk_matmul(): pl.pallas_call(kernel, out_shape=jax.ShapeDtypeStruct((rows, outs), out_t...  29.1 us
    all_to_all x2, waiting for transfers between devices, on_device(): lax.all_to_all(low, 'tensor', 0, 0, axis_index_groups=Z_GROUPS, tiled=True)  14.2 us
    ppermute x23, waiting for transfers between devices, move(): return lax.ppermute(value, 'tensor', perm)  12.9 us
    all_to_all x2, starting transfers between devices, on_device(): lax.all_to_all(low, 'tensor', 0, 0, axis_index_groups=Z_GROUPS, tiled=True)  9.55 us
    all_to_all x1, starting transfers between devices, on_device(): got = lax.all_to_all(sent, 'dp', 0, 0, tiled=True)  5.12 us
  transfers between devices with their start and end apart: 26, of which 10 were waited for; matrix products, arithmetic and copies ran while one was open for 8% of the time, Pallas kernels for 17%

profile of v2, /device:TPU:1, one launch (start us, length us, event | category | flops | bytes accessed | tf_op | source)
XLA Modules:
  0.0 120.7 jit_solution(7012952968104951318)
XLA Ops:
  0.6 0.0 copy-start
  0.7 3.3 %collective-permute-start.7 = (bf16[768,256]{1,0:T(8,128)(2,1)}, bf16[768,256]{1,0:T(8,128)(2,1)S(1)}, u32[]{:S(2)}, u32[]{:S(2)}) collective-permute-start(bf16[768,256]{1,0:T(8,128)(2,1)} %param.8), channel_id=1, source_target_pairs={{0,1},{1,0},{2,3},{3,2},{4,5},{5,4},{6,7},{7,6},{8,9},{9,8},{10,11... | collective-permute-start | bytes 1179656 | tf_op jit(solution)/shard_map/ppermute | solution.py:35
  4.0 1.0 collective-permute-start
  5.0 0.5 collective-permute-done.7
  5.6 1.3 %maximum_select_fusion.1.refs_0_ = bf16[768,512]{1,0:T(8,128)(2,1)S(1)} fusion(bf16[768,256]{1,0:T(8,128)(2,1)S(1)} %collective-permute-done.7, bf16[768,256]{1,0:T(8,128)(2,1)} %param.8, pred[]{:T(512)S(6)} %eq.21), kind=kLoop, calls=%fused_computation.2 | loop fusion | flops 3538944 | bytes 1572865 | tf_op jit(solution)/shard_map/jit(_where)/select_n | solution.py:131
  6.9 5.1 %collective-permute-start.8 = (bf16[768,512]{1,0:T(8,128)(2,1)S(1)}, bf16[768,512]{1,0:T(8,128)(2,1)}, u32[]{:S(2)}, u32[]{:S(2)}) collective-permute-start(bf16[768,512]{1,0:T(8,128)(2,1)S(1)} %maximum_select_fusion.1.refs_0_), channel_id=1, source_target_pairs={{0,2},{1,15},{2,4},{3,1},{4,6},{5,3},{6,8},{7,5},{8,10},{9,7},{10,... | collective-permute-start | bytes 2359304 | tf_op jit(solution)/shard_map/ppermute | solution.py:35
  12.0 4.4 %collective-permute-done = bf16[768,256]{1,0:T(8,128)(2,1)S(1)} collective-permute-done((bf16[768,256]{1,0:T(8,128)(2,1)}, bf16[768,256]{1,0:T(8,128)(2,1)S(1)}, u32[]{:S(2)}, u32[]{:S(2)}) %collective-permute-start) | collective-permute-done | bytes 393248 | tf_op jit(solution)/shard_map/ppermute | solution.py:35
  16.4 0.9 collective-permute-start.1
  17.3 0.4 fusion.6
  17.7 0.0 copy-done.5
  17.7 0.3 convolution_bitcast_fusion
  18.0 0.6 collective-permute-done.1
  18.6 0.2 maximum_select_fusion.refs_1_
  18.8 0.0 copy-start.11
  18.9 3.9 %collective-permute-start.2 = (bf16[768,512]{1,0:T(8,128)(2,1)S(1)}, bf16[768,512]{1,0:T(8,128)(2,1)}, u32[]{:S(2)}, u32[]{:S(2)}) collective-permute-start(bf16[768,512]{1,0:T(8,128)(2,1)S(1)} %maximum_select_fusion.refs_1_), channel_id=1, source_target_pairs={{0,2},{1,15},{2,4},{3,1},{4,6},{5,3},{6,8},{7,5},{8,10},{9,7},{10,... | collective-permute-start | bytes 2359304 | tf_op jit(solution)/shard_map/ppermute | solution.py:35
  22.8 0.2 copy.16
  23.0 0.1 collective-permute-start.12
  23.1 0.0 collective-permute-done.8.refs_2_
  23.1 1.0 collective-permute-start.9
  24.2 0.4 collective-permute-done.12
  24.6 2.8 %collective-permute-start.13 = (f32[3,64,128]{2,1,0:T(8,128)S(1)}, f32[3,64,128]{2,1,0:T(8,128)S(1)}, u32[]{:S(2)}, u32[]{:S(2)}) collective-permute-start(f32[3,64,128]{2,1,0:T(8,128)S(1)} %constant_dynamic-slice_fusion), channel_id=1, source_target_pairs={{0,16},{1,17},{2,18},{3,19},{4,20},{5,21},{6,22},{7,23},{8,24},{9,... | collective-permute-start | bytes 294920 | tf_op jit(solution)/shard_map/ppermute | solution.py:35
  27.4 4.3 %collective-permute-done.2.refs_4_ = bf16[768,512]{1,0:T(8,128)(2,1)} collective-permute-done((bf16[768,512]{1,0:T(8,128)(2,1)S(1)}, bf16[768,512]{1,0:T(8,128)(2,1)}, u32[]{:S(2)}, u32[]{:S(2)}) %collective-permute-start.2) | collective-permute-done | bytes 786464 | tf_op jit(solution)/shard_map/ppermute | solution.py:35
  31.7 3.2 %collective-permute-start.3 = (bf16[768,512]{1,0:T(8,128)(2,1)}, bf16[768,512]{1,0:T(8,128)(2,1)}, u32[]{:S(2)}, u32[]{:S(2)}) collective-permute-start(bf16[768,512]{1,0:T(8,128)(2,1)} %collective-permute-done.2.refs_4_), channel_id=1, source_target_pairs={{0,2},{1,15},{2,4},{3,1},{4,6},{5,3},{6,8},{7,5},{8,10},{9,7},{10,... | collective-permute-start | bytes 2359304 | tf_op jit(solution)/shard_map/ppermute | solution.py:35
  35.0 0.6 copy.17
  35.6 3.4 %all-to-all-start = ((f32[8,3,8,128]{3,2,1,0:T(8,128)}), f32[8,3,8,128]{3,2,1,0:T(8,128)S(1)}, u32[]{:S(2)}, u32[]{:S(2)}) async-start(f32[8,3,8,128]{3,2,1,0:T(8,128)} %copy.17), calls=%async_computation | async-start | bytes 196608 | tf_op jit(solution)/shard_map/all_to_all | solution.py:181
  39.0 0.1 dynamic_slice.23
  39.1 0.7 stack.83.blocks_ref
  39.7 10.9 %all-to-all-done = f32[8,3,8,128]{3,2,1,0:T(8,128)S(1)} async-done(((f32[8,3,8,128]{3,2,1,0:T(8,128)}), f32[8,3,8,128]{3,2,1,0:T(8,128)S(1)}, u32[]{:S(2)}, u32[]{:S(2)}) %all-to-all-start) | async-done | bytes 98336 | tf_op jit(solution)/shard_map/all_to_all | solution.py:181
  50.7 0.6 broadcast_in_dim.2
  51.3 6.2 %all-to-all-start.1 = ((f32[8,3,8,128]{3,2,1,0:T(8,128)}), f32[8,3,8,128]{3,2,1,0:T(8,128)S(1)}, u32[]{:S(2)}, u32[]{:S(2)}) async-start(f32[8,3,8,128]{3,2,1,0:T(8,128)} %broadcast_in_dim.2), calls=%async_computation.1 | async-start | bytes 196608 | tf_op jit(solution)/shard_map/all_to_all | solution.py:189
  57.5 1.3 %collective-permute-start.14 = (bf16[768,512]{1,0:T(8,128)(2,1)}, bf16[768,512]{1,0:T(8,128)(2,1)}, u32[]{:S(2)}, u32[]{:S(2)}) collective-permute-start(bf16[768,512]{1,0:T(8,128)(2,1)} %collective-permute-done.8.refs_2_), channel_id=1, source_target_pairs={{0,1},{1,0},{2,3},{3,2},{4,5},{5,4},{6,7},{7,6},{8,9},{9,8},{10,11... | collective-permute-start | bytes 2359304 | tf_op jit(solution)/shard_map/ppermute | solution.py:35
  58.9 0.1 collective-permute-start.15
  59.0 2.9 %collective-permute-start.10 = (bf16[768,512]{1,0:T(8,128)(2,1)}, bf16[768,512]{1,0:T(8,128)(2,1)S(1)}, u32[]{:S(2)}, u32[]{:S(2)}) collective-permute-start(bf16[768,512]{1,0:T(8,128)(2,1)} %collective-permute-done.9.refs_0_), channel_id=1, source_target_pairs={{0,2},{1,15},{2,4},{3,1},{4,6},{5,3},{6,8},{7,5},{8,10},{9,7},{10,... | collective-permute-start | bytes 2359304 | tf_op jit(solution)/shard_map/ppermute | solution.py:35
  61.8 0.1 fusion.5
  61.9 3.2 %all-to-all-done.1 = f32[8,3,8,128]{3,2,1,0:T(8,128)S(1)} async-done(((f32[8,3,8,128]{3,2,1,0:T(8,128)}), f32[8,3,8,128]{3,2,1,0:T(8,128)S(1)}, u32[]{:S(2)}, u32[]{:S(2)}) %all-to-all-start.1) | async-done | bytes 98336 | tf_op jit(solution)/shard_map/all_to_all | solution.py:189
  65.1 2.7 %collective-permute-start.16 = (bf16[768,512]{1,0:T(8,128)(2,1)}, bf16[768,512]{1,0:T(8,128)(2,1)}, u32[]{:S(2)}, u32[]{:S(2)}) collective-permute-start(bf16[768,512]{1,0:T(8,128)(2,1)} %collective-permute-done.9.refs_0_), channel_id=1, source_target_pairs={{0,1},{1,0},{2,3},{3,2},{4,5},{5,4},{6,7},{7,6},{8,9},{9,8},{10,11... | collective-permute-start | bytes 2359304 | tf_op jit(solution)/shard_map/ppermute | solution.py:35
  67.8 0.6 collective-permute-start.4
  68.4 0.4 fusion
  68.8 0.1 mul.143
  68.9 0.1 multiply_reduce_fusion
  69.0 0.9 reshape.40
  69.9 5.1 %all-to-all-start.2 = ((f32[8,2,4096]{2,1,0:T(2,128)}), f32[8,2,4096]{2,1,0:T(2,128)S(1)}, u32[]{:S(2)}, u32[]{:S(2)}) async-start(f32[8,2,4096]{2,1,0:T(2,128)} %reshape.40), calls=%async_computation.2 | async-start | bytes 524288 | tf_op jit(solution)/shard_map/all_to_all | solution.py:205
  75.0 0.6 collective-permute-start.19
  75.6 0.3 collective-permute-start.20
  75.9 9.5 %chunk_matmul.3.refs_7_ = f32[768,640]{1,0:T(8,128)} custom-call(s32[6]{0:T(128)} %stack.83.blocks_ref, bf16[768,512]{1,0:T(8,128)(2,1)} %copy-done.1, bf16[768,512]{1,0:T(8,128)(2,1)} %copy-done.2, bf16[768,512]{1,0:T(8,128)(2,1)} %collective-permute-done.8.refs_2_, bf16[768,512]{1,0:T(8,128)(2,1)} %collective-permute-done.14.refs_3_, ...), custom_call_target="tpu_custom_call" | custom-call | flops 3019898880 | bytes 12582912 | tf_op jit(solution)/shard_map/chunk_matmul/pallas_call | solution.py:98
  85.4 0.1 reduce_sum.29
  85.5 2.5 %collective-permute-start.17 = (f32[2,4096]{1,0:T(2,128)S(1)}, f32[2,4096]{1,0:T(2,128)S(1)}, u32[]{:S(2)}, u32[]{:S(2)}) collective-permute-start(f32[2,4096]{1,0:T(2,128)S(1)} %reduce_sum.29), channel_id=1, source_target_pairs={{0,16},{1,17},{2,18},{3,19},{4,20},{5,21},{6,22},{7,23},{8,24},{9,... | collective-permute-start | bytes 98312 | tf_op jit(solution)/shard_map/ppermute | solution.py:35
  88.1 0.6 stack.76.blocks_ref
  88.7 1.2 %collective-permute-done.17 = f32[2,4096]{1,0:T(2,128)S(1)} collective-permute-done((f32[2,4096]{1,0:T(2,128)S(1)}, f32[2,4096]{1,0:T(2,128)S(1)}, u32[]{:S(2)}, u32[]{:S(2)}) %collective-permute-start.17) | collective-permute-done | bytes 32800 | tf_op jit(solution)/shard_map/ppermute | solution.py:35
  89.9 1.5 %collective-permute-start.18 = (f32[2,4096]{1,0:T(2,128)S(1)}, f32[2,4096]{1,0:T(2,128)S(1)}, u32[]{:S(2)}, u32[]{:S(2)}) collective-permute-start(f32[2,4096]{1,0:T(2,128)S(1)} %add.178), channel_id=1, source_target_pairs={{0,1},{1,0},{2,3},{3,2},{4,5},{5,4},{6,7},{7,6},{8,9},{9,8},{10,11... | collective-permute-start | bytes 98312 | tf_op jit(solution)/shard_map/ppermute | solution.py:35
  91.4 2.3 %collective-permute-start.11 = (bf16[768,256]{1,0:T(8,128)(2,1)S(1)}, bf16[768,256]{1,0:T(8,128)(2,1)}, u32[]{:S(2)}, u32[]{:S(2)}) collective-permute-start(bf16[768,256]{1,0:T(8,128)(2,1)S(1)} %constant_dynamic-slice_fusion.2), channel_id=1, source_target_pairs={{0,2},{1,15},{2,4},{3,1},{4,6},{5,3},{6,8},{7,5},{8,10},{9,7},{10,... | collective-permute-start | bytes 1179656 | tf_op jit(solution)/shard_map/ppermute | solution.py:35
  93.7 0.8 constant_dynamic-slice_fusion.3
  94.5 0.2 collective-permute-start.6
  94.7 1.8 %fusion.3 = f32[2,32]{1,0:T(2,128)} fusion(bf16[32,4096]{1,0:T(8,128)(2,1)} %param.12, f32[2,4096]{1,0:T(2,128)S(1)} %add.178, f32[2,4096]{1,0:T(2,128)S(1)} %collective-permute-done.18), kind=kOutput, calls=%fused_computation.11 | convolution fusion | flops 3153920 | bytes 327936 | tf_op jit(solution)/shard_map/dot_general | solution.py:223
  96.5 11.0 %chunk_matmul.4.refs_7_ = f32[768,640]{1,0:T(8,128)} custom-call(s32[6]{0:T(128)} %stack.76.blocks_ref, bf16[768,512]{1,0:T(8,128)(2,1)} %collective-permute-done.9.refs_0_, bf16[768,512]{1,0:T(8,128)(2,1)} %collective-permute-done.16.refs_1_, bf16[768,512]{1,0:T(8,128)(2,1)} %collective-permute-done.3.refs_2_, ...), custom_call_target="tpu_custom_call" | custom-call | flops 3019898880 | bytes 12582912 | tf_op jit(solution)/shard_map/chunk_matmul/pallas_call | solution.py:98
  107.5 0.6 collective-permute-start.21
  108.1 0.1 collective-permute-start.22
  108.2 0.6 stack.69.blocks_ref
  108.8 0.9 collective-permute-done.21.refs_3_
  109.6 0.6 collective-permute-done.22.refs_5_
  110.2 0.2 copy-done.7
  110.4 0.5 copy-done.8
  111.0 0.9 copy-done.6
  111.9 8.6 %chunk_matmul.5 = bf16[768,640]{1,0:T(8,128)(2,1)} custom-call(s32[6]{0:T(128)} %stack.69.blocks_ref, bf16[768,512]{1,0:T(8,128)(2,1)} %copy-done.3, bf16[768,512]{1,0:T(8,128)(2,1)} %copy-done.6, bf16[768,256]{1,0:T(8,128)(2,1)} %collective-permute-done.11.refs_2_, bf16[768,256]{1,0:T(8,128)(2,1)} %copy-done.7, ...), custom_call_target="tpu_custom_call" | custom-call | flops 2013265920 | bytes 9699328 | tf_op jit(solution)/shard_map/chunk_matmul/pallas_call | solution.py:98
  (43 shorter events, 0.2 us)
Async XLA Ops:
  0.6 16.6 %copy-start = (bf16[768,640]{1,0:T(8,128)(2,1)S(1)}, bf16[768,640]{1,0:T(8,128)(2,1)}, u32[]{:S(2)}) copy-start(bf16[768,640]{1,0:T(8,128)(2,1)} %param.7) | copy-start | bytes 2949124
  0.6 17.0 %copy-start.5 = (bf16[768,256]{1,0:T(8,128)(2,1)S(1)}, bf16[768,256]{1,0:T(8,128)(2,1)}, u32[]{:S(2)}) copy-start(bf16[768,256]{1,0:T(8,128)(2,1)} %param.8) | copy-start | bytes 1179652
  0.7 17.0 %copy-start.10 = (bf16[64,256]{1,0:T(8,128)(2,1)S(1)}, bf16[64,256]{1,0:T(8,128)(2,1)}, u32[]{:S(2)}) copy-start(bf16[64,256]{1,0:T(8,128)(2,1)} %param.11) | copy-start | bytes 98308
  0.7 16.6 %copy-start.9 = (bf16[64,640]{1,0:T(8,128)(2,1)S(1)}, bf16[64,640]{1,0:T(8,128)(2,1)}, u32[]{:S(2)}) copy-start(bf16[64,640]{1,0:T(8,128)(2,1)} %param.10) | copy-start | bytes 245764
  0.7 4.9 %collective-permute-start.7 = (bf16[768,256]{1,0:T(8,128)(2,1)}, bf16[768,256]{1,0:T(8,128)(2,1)S(1)}, u32[]{:S(2)}, u32[]{:S(2)}) collective-permute-start(bf16[768,256]{1,0:T(8,128)(2,1)} %param.8), channel_id=1, source_target_pairs={{0,1},{1,0},{2,3},{3,2},{4,5},{5,4},{6,7},{7,6},{8,9},{9,8},{10,11... | collective-permute-start | bytes 1179656 | tf_op jit(solution)/shard_map/ppermute | solution.py:35
  4.0 12.4 %collective-permute-start = (bf16[768,256]{1,0:T(8,128)(2,1)}, bf16[768,256]{1,0:T(8,128)(2,1)S(1)}, u32[]{:S(2)}, u32[]{:S(2)}) collective-permute-start(bf16[768,256]{1,0:T(8,128)(2,1)} %param.8), channel_id=1, source_target_pairs={{0,16},{1,17},{2,18},{3,19},{4,20},{5,21},{6,22},{7,23},{8,24},{9,... | collective-permute-start | bytes 1179656 | tf_op jit(solution)/shard_map/ppermute | solution.py:35
  6.9 12.0 %copy-start.1 = (bf16[768,512]{1,0:T(8,128)(2,1)}, bf16[768,512]{1,0:T(8,128)(2,1)S(1)}, u32[]{:S(2)}) copy-start(bf16[768,512]{1,0:T(8,128)(2,1)S(1)} %maximum_select_fusion.1.refs_0_) | copy-start | bytes 2359300
  6.9 16.2 %collective-permute-start.8 = (bf16[768,512]{1,0:T(8,128)(2,1)S(1)}, bf16[768,512]{1,0:T(8,128)(2,1)}, u32[]{:S(2)}, u32[]{:S(2)}) collective-permute-start(bf16[768,512]{1,0:T(8,128)(2,1)S(1)} %maximum_select_fusion.1.refs_0_), channel_id=1, source_target_pairs={{0,2},{1,15},{2,4},{3,1},{4,6},{5,3},{6,8},{7,5},{8,10},{9,7},{10,... | collective-permute-start | bytes 2359304 | tf_op jit(solution)/shard_map/ppermute | solution.py:35
  16.4 2.2 %collective-permute-start.1 = (bf16[768,256]{1,0:T(8,128)(2,1)S(1)}, bf16[768,256]{1,0:T(8,128)(2,1)S(1)}, u32[]{:S(2)}, u32[]{:S(2)}) collective-permute-start(bf16[768,256]{1,0:T(8,128)(2,1)S(1)} %collective-permute-done), channel_id=1, source_target_pairs={{0,1},{1,0},{2,3},{3,2},{4,5},{5,4},{6,7},{7,6},{8,9},{9,8},{10,11... | collective-permute-start | bytes 1179656 | tf_op jit(solution)/shard_map/ppermute | solution.py:35
  18.8 16.8 %copy-start.2 = (bf16[768,512]{1,0:T(8,128)(2,1)}, bf16[768,512]{1,0:T(8,128)(2,1)S(1)}, u32[]{:S(2)}) copy-start(bf16[768,512]{1,0:T(8,128)(2,1)S(1)} %maximum_select_fusion.refs_1_) | copy-start | bytes 2359300
  18.8 20.2 %copy-start.11 = (s32[24]{0:T(128)S(1)}, s32[24]{0:T(128)}, u32[]{:S(2)}) copy-start(s32[24]{0:T(128)} %param.13) | copy-start | bytes 292
  18.9 12.9 %collective-permute-start.2 = (bf16[768,512]{1,0:T(8,128)(2,1)S(1)}, bf16[768,512]{1,0:T(8,128)(2,1)}, u32[]{:S(2)}, u32[]{:S(2)}) collective-permute-start(bf16[768,512]{1,0:T(8,128)(2,1)S(1)} %maximum_select_fusion.refs_1_), channel_id=1, source_target_pairs={{0,2},{1,15},{2,4},{3,1},{4,6},{5,3},{6,8},{7,5},{8,10},{9,7},{10,... | collective-permute-start | bytes 2359304 | tf_op jit(solution)/shard_map/ppermute | solution.py:35
  23.0 1.5 %collective-permute-start.12 = (f32[3,128,128]{2,1,0:T(8,128)S(1)}, f32[3,128,128]{2,1,0:T(8,128)S(1)}, u32[]{:S(2)}, u32[]{:S(2)}) collective-permute-start(f32[3,128,128]{2,1,0:T(8,128)S(1)} %constant_dynamic-slice_fusion.1), channel_id=1, source_target_pairs={{0,1},{1,0},{2,3},{3,2},{4,5},{5,4},{6,7},{7,6},{8,9},{9,8},{10,11... | collective-permute-start | bytes 589832 | tf_op jit(solution)/shard_map/ppermute | solution.py:35
  23.1 35.8 %collective-permute-start.9 = (bf16[768,512]{1,0:T(8,128)(2,1)}, bf16[768,512]{1,0:T(8,128)(2,1)}, u32[]{:S(2)}, u32[]{:S(2)}) collective-permute-start(bf16[768,512]{1,0:T(8,128)(2,1)} %collective-permute-done.8.refs_2_), channel_id=1, source_target_pairs={{0,2},{1,15},{2,4},{3,1},{4,6},{5,3},{6,8},{7,5},{8,10},{9,7},{10,... | collective-permute-start | bytes 2359304 | tf_op jit(solution)/shard_map/ppermute | solution.py:35
  24.6 10.4 %collective-permute-start.13 = (f32[3,64,128]{2,1,0:T(8,128)S(1)}, f32[3,64,128]{2,1,0:T(8,128)S(1)}, u32[]{:S(2)}, u32[]{:S(2)}) collective-permute-start(f32[3,64,128]{2,1,0:T(8,128)S(1)} %constant_dynamic-slice_fusion), channel_id=1, source_target_pairs={{0,16},{1,17},{2,18},{3,19},{4,20},{5,21},{6,22},{7,23},{8,24},{9,... | collective-permute-start | bytes 294920 | tf_op jit(solution)/shard_map/ppermute | solution.py:35
  31.7 36.1 %collective-permute-start.3 = (bf16[768,512]{1,0:T(8,128)(2,1)}, bf16[768,512]{1,0:T(8,128)(2,1)}, u32[]{:S(2)}, u32[]{:S(2)}) collective-permute-start(bf16[768,512]{1,0:T(8,128)(2,1)} %collective-permute-done.2.refs_4_), channel_id=1, source_target_pairs={{0,2},{1,15},{2,4},{3,1},{4,6},{5,3},{6,8},{7,5},{8,10},{9,7},{10,... | collective-permute-start | bytes 2359304 | tf_op jit(solution)/shard_map/ppermute | solution.py:35
  35.6 15.1 %all-to-all-start = ((f32[8,3,8,128]{3,2,1,0:T(8,128)}), f32[8,3,8,128]{3,2,1,0:T(8,128)S(1)}, u32[]{:S(2)}, u32[]{:S(2)}) async-start(f32[8,3,8,128]{3,2,1,0:T(8,128)} %copy.17), calls=%async_computation | async-start | bytes 196608 | tf_op jit(solution)/shard_map/all_to_all | solution.py:181
  51.3 13.8 %all-to-all-start.1 = ((f32[8,3,8,128]{3,2,1,0:T(8,128)}), f32[8,3,8,128]{3,2,1,0:T(8,128)S(1)}, u32[]{:S(2)}, u32[]{:S(2)}) async-start(f32[8,3,8,128]{3,2,1,0:T(8,128)} %broadcast_in_dim.2), calls=%async_computation.1 | async-start | bytes 196608 | tf_op jit(solution)/shard_map/all_to_all | solution.py:189
  57.5 17.5 %collective-permute-start.14 = (bf16[768,512]{1,0:T(8,128)(2,1)}, bf16[768,512]{1,0:T(8,128)(2,1)}, u32[]{:S(2)}, u32[]{:S(2)}) collective-permute-start(bf16[768,512]{1,0:T(8,128)(2,1)} %collective-permute-done.8.refs_2_), channel_id=1, source_target_pairs={{0,1},{1,0},{2,3},{3,2},{4,5},{5,4},{6,7},{7,6},{8,9},{9,8},{10,11... | collective-permute-start | bytes 2359304 | tf_op jit(solution)/shard_map/ppermute | solution.py:35
  58.9 17.0 %collective-permute-start.15 = (bf16[768,512]{1,0:T(8,128)(2,1)}, bf16[768,512]{1,0:T(8,128)(2,1)}, u32[]{:S(2)}, u32[]{:S(2)}) collective-permute-start(bf16[768,512]{1,0:T(8,128)(2,1)} %collective-permute-done.2.refs_4_), channel_id=1, source_target_pairs={{0,1},{1,0},{2,3},{3,2},{4,5},{5,4},{6,7},{7,6},{8,9},{9,8},{10,11... | collective-permute-start | bytes 2359304 | tf_op jit(solution)/shard_map/ppermute | solution.py:35
  59.0 16.6 %collective-permute-start.10 = (bf16[768,512]{1,0:T(8,128)(2,1)}, bf16[768,512]{1,0:T(8,128)(2,1)S(1)}, u32[]{:S(2)}, u32[]{:S(2)}) collective-permute-start(bf16[768,512]{1,0:T(8,128)(2,1)} %collective-permute-done.9.refs_0_), channel_id=1, source_target_pairs={{0,2},{1,15},{2,4},{3,1},{4,6},{5,3},{6,8},{7,5},{8,10},{9,7},{10,... | collective-permute-start | bytes 2359304 | tf_op jit(solution)/shard_map/ppermute | solution.py:35
  65.1 29.5 %collective-permute-start.16 = (bf16[768,512]{1,0:T(8,128)(2,1)}, bf16[768,512]{1,0:T(8,128)(2,1)}, u32[]{:S(2)}, u32[]{:S(2)}) collective-permute-start(bf16[768,512]{1,0:T(8,128)(2,1)} %collective-permute-done.9.refs_0_), channel_id=1, source_target_pairs={{0,1},{1,0},{2,3},{3,2},{4,5},{5,4},{6,7},{7,6},{8,9},{9,8},{10,11... | collective-permute-start | bytes 2359304 | tf_op jit(solution)/shard_map/ppermute | solution.py:35
  67.8 23.6 %collective-permute-start.4 = (bf16[768,512]{1,0:T(8,128)(2,1)}, bf16[768,512]{1,0:T(8,128)(2,1)S(1)}, u32[]{:S(2)}, u32[]{:S(2)}) collective-permute-start(bf16[768,512]{1,0:T(8,128)(2,1)} %collective-permute-done.3.refs_2_), channel_id=1, source_target_pairs={{0,2},{1,15},{2,4},{3,1},{4,6},{5,3},{6,8},{7,5},{8,10},{9,7},{10,... | collective-permute-start | bytes 2359304 | tf_op jit(solution)/shard_map/ppermute | solution.py:35
  69.9 15.6 %all-to-all-start.2 = ((f32[8,2,4096]{2,1,0:T(2,128)}), f32[8,2,4096]{2,1,0:T(2,128)S(1)}, u32[]{:S(2)}, u32[]{:S(2)}) async-start(f32[8,2,4096]{2,1,0:T(2,128)} %reshape.40), calls=%async_computation.2 | async-start | bytes 524288 | tf_op jit(solution)/shard_map/all_to_all | solution.py:205
  75.0 21.5 %collective-permute-start.19 = (bf16[768,512]{1,0:T(8,128)(2,1)}, bf16[768,512]{1,0:T(8,128)(2,1)}, u32[]{:S(2)}, u32[]{:S(2)}) collective-permute-start(bf16[768,512]{1,0:T(8,128)(2,1)} %collective-permute-done.3.refs_2_), channel_id=1, source_target_pairs={{0,1},{1,0},{2,3},{3,2},{4,5},{5,4},{6,7},{7,6},{8,9},{9,8},{10,11... | collective-permute-start | bytes 2359304 | tf_op jit(solution)/shard_map/ppermute | solution.py:35
  75.6 15.8 %copy-start.4 = (bf16[768,512]{1,0:T(8,128)(2,1)}, bf16[768,512]{1,0:T(8,128)(2,1)S(1)}, u32[]{:S(2)}) copy-start(bf16[768,512]{1,0:T(8,128)(2,1)S(1)} %collective-permute-done.10.refs_4_) | copy-start | bytes 2359300
  75.6 20.9 %collective-permute-start.20 = (bf16[768,512]{1,0:T(8,128)(2,1)S(1)}, bf16[768,512]{1,0:T(8,128)(2,1)}, u32[]{:S(2)}, u32[]{:S(2)}) collective-permute-start(bf16[768,512]{1,0:T(8,128)(2,1)S(1)} %collective-permute-done.10.refs_4_), channel_id=1, source_target_pairs={{0,1},{1,0},{2,3},{3,2},{4,5},{5,4},{6,7},{7,6},{8,9},{9,8},{10,11... | collective-permute-start | bytes 2359304 | tf_op jit(solution)/shard_map/ppermute | solution.py:35
  85.5 4.4 %collective-permute-start.17 = (f32[2,4096]{1,0:T(2,128)S(1)}, f32[2,4096]{1,0:T(2,128)S(1)}, u32[]{:S(2)}, u32[]{:S(2)}) collective-permute-start(f32[2,4096]{1,0:T(2,128)S(1)} %reduce_sum.29), channel_id=1, source_target_pairs={{0,16},{1,17},{2,18},{3,19},{4,20},{5,21},{6,22},{7,23},{8,24},{9,... | collective-permute-start | bytes 98312 | tf_op jit(solution)/shard_map/ppermute | solution.py:35
  89.9 4.6 %collective-permute-start.18 = (f32[2,4096]{1,0:T(2,128)S(1)}, f32[2,4096]{1,0:T(2,128)S(1)}, u32[]{:S(2)}, u32[]{:S(2)}) collective-permute-start(f32[2,4096]{1,0:T(2,128)S(1)} %add.178), channel_id=1, source_target_pairs={{0,1},{1,0},{2,3},{3,2},{4,5},{5,4},{6,7},{7,6},{8,9},{9,8},{10,11... | collective-permute-start | bytes 98312 | tf_op jit(solution)/shard_map/ppermute | solution.py:35
  91.4 16.0 %copy-start.3 = (bf16[768,512]{1,0:T(8,128)(2,1)}, bf16[768,512]{1,0:T(8,128)(2,1)S(1)}, u32[]{:S(2)}) copy-start(bf16[768,512]{1,0:T(8,128)(2,1)S(1)} %collective-permute-done.4.refs_0_) | copy-start | bytes 2359300
  91.4 16.0 %collective-permute-start.11 = (bf16[768,256]{1,0:T(8,128)(2,1)S(1)}, bf16[768,256]{1,0:T(8,128)(2,1)}, u32[]{:S(2)}, u32[]{:S(2)}) collective-permute-start(bf16[768,256]{1,0:T(8,128)(2,1)S(1)} %constant_dynamic-slice_fusion.2), channel_id=1, source_target_pairs={{0,2},{1,15},{2,4},{3,1},{4,6},{5,3},{6,8},{7,5},{8,10},{9,7},{10,... | collective-permute-start | bytes 1179656 | tf_op jit(solution)/shard_map/ppermute | solution.py:35
  94.5 13.0 %collective-permute-start.6 = (bf16[768,256]{1,0:T(8,128)(2,1)}, bf16[768,256]{1,0:T(8,128)(2,1)}, u32[]{:S(2)}, u32[]{:S(2)}) collective-permute-start(bf16[768,256]{1,0:T(8,128)(2,1)} %constant_dynamic-slice_fusion.3), channel_id=1, source_target_pairs={{0,2},{1,15},{2,4},{3,1},{4,6},{5,3},{6,8},{7,5},{8,10},{9,7},{10,... | collective-permute-start | bytes 1179656 | tf_op jit(solution)/shard_map/ppermute | solution.py:35
  94.6 15.6 %collective-permute-start.5 = (bf16[768,512]{1,0:T(8,128)(2,1)S(1)}, bf16[768,512]{1,0:T(8,128)(2,1)S(1)}, u32[]{:S(2)}, u32[]{:S(2)}) collective-permute-start(bf16[768,512]{1,0:T(8,128)(2,1)S(1)} %collective-permute-done.4.refs_0_), channel_id=1, source_target_pairs={{0,1},{1,0},{2,3},{3,2},{4,5},{5,4},{6,7},{7,6},{8,9},{9,8},{10,11... | collective-permute-start | bytes 2359304 | tf_op jit(solution)/shard_map/ppermute | solution.py:35
  107.5 2.2 %collective-permute-start.21 = (bf16[768,256]{1,0:T(8,128)(2,1)}, bf16[768,256]{1,0:T(8,128)(2,1)S(1)}, u32[]{:S(2)}, u32[]{:S(2)}) collective-permute-start(bf16[768,256]{1,0:T(8,128)(2,1)} %collective-permute-done.11.refs_2_), channel_id=1, source_target_pairs={{0,1},{1,0},{2,3},{3,2},{4,5},{5,4},{6,7},{7,6},{8,9},{9,8},{10,11... | collective-permute-start | bytes 1179656 | tf_op jit(solution)/shard_map/ppermute | solution.py:35
  108.1 2.1 %collective-permute-start.22 = (bf16[768,256]{1,0:T(8,128)(2,1)}, bf16[768,256]{1,0:T(8,128)(2,1)S(1)}, u32[]{:S(2)}, u32[]{:S(2)}) collective-permute-start(bf16[768,256]{1,0:T(8,128)(2,1)} %collective-permute-done.6.refs_4_), channel_id=1, source_target_pairs={{0,1},{1,0},{2,3},{3,2},{4,5},{5,4},{6,7},{7,6},{8,9},{9,8},{10,11... | collective-permute-start | bytes 1179656 | tf_op jit(solution)/shard_map/ppermute | solution.py:35
  109.6 0.8 copy-start.7
  110.2 0.7 copy-start.8
  111.0 0.9 copy-start.6
